TPU v7x, 128 devices: a whole 4x4x4 slice. The times are simulated.
128 devices in a mesh: chan: 32 (over z_lo, y, x), seg: 4 (over z_hi, core).
Axes of the slice: x: 4, y: 4, z: 4 (z_hi: 2, z_lo: 2; z = z_hi * 2 + z_lo), core: 2. Of those that a mesh axis runs over, the one named last changes fastest.
Arguments:
- traces: bfloat16 [4096, 8, 8192], P('chan', 'seg'), may hold values from -20 to 20
- pair_offsets: int32 [32, 16], replicated, may hold values from 1 to 31, as said below
- pair_counts: int32 [32], replicated, may hold values from 1 to 16, 64 in all
- pair_owner: int32 [64], replicated, may hold values from 0 to 63, each once
Outputs:
- correlations: float32 [128, 64, 128, 256], P('seg', 'chan')
Inputs may be any that keep to these rules, and one draw needn't show every extreme that they name: `pair_offsets`: row a lists 16 distinct offsets; only its first pair_counts[a] entries name pairs. `pair_counts`: the counts sum to 64. `pair_owner`: every slot number appears once.
All inputs are finite; a program needn't handle non-finite values.
Results may differ from a plain program's by a relative error of at most 0.017.
Values may be sent and summed in bfloat16 or wider, within the bound.
No kernel may reach another device: no remote copies, remote signals or barrier semaphores. Data moves between devices by JAX's collectives and lax.ppermute only.
A program may use at most 128 MiB of HBM per device.

v0:
```python
import math

import jax
import jax.numpy as jnp
from jax import lax
from jax.sharding import PartitionSpec as P

SAMPLES = 8192
BAND_START = 32
FREQS = 512
HALF = 8
LAGS = 256
TILE_DEV = 2


def smoother(bin_count):
    bins_axis = lax.iota(jnp.int32, bin_count)
    nearby = (jnp.abs(bins_axis[:, None] - bins_axis[None, :]) <= HALF).astype(jnp.float32)
    return nearby / jnp.sum(nearby, axis=0, keepdims=True)


def lag_table(first_bin, bin_count):
    bins_axis = BAND_START + first_bin + lax.iota(jnp.int32, bin_count)
    shifts = jnp.mod(lax.iota(jnp.int32, LAGS) - LAGS // 2, SAMPLES)
    phase_index = jnp.mod(bins_axis[:, None] * shifts[None, :], SAMPLES)
    angles = phase_index.astype(jnp.float32) * (2.0 * math.pi / SAMPLES)
    return jnp.concatenate([jnp.cos(angles), -jnp.sin(angles)], axis=0).astype(jnp.bfloat16)


def pair_blocks(pair_offsets, pair_counts, pair_owner, block_count, slot_count):
    slot_index = lax.iota(jnp.int32, slot_count)
    starts = jnp.cumsum(pair_counts) - pair_counts
    first_block = jnp.sum((starts[None, :] <= slot_index[:, None]).astype(jnp.int32), axis=1) - 1
    member = lax.iota(jnp.int32, block_count)[None, :] == first_block[:, None]
    start_of = jnp.sum(jnp.where(member, starts[None, :], 0), axis=1)
    position = slot_index - start_of
    listed = jnp.sum(jnp.where(member[:, :, None], pair_offsets[None, :, :], 0), axis=1)
    chosen = lax.iota(jnp.int32, pair_offsets.shape[1])[None, :] == position[:, None]
    offset = jnp.sum(jnp.where(chosen, listed, 0), axis=1)
    second_block = jnp.mod(first_block + offset, block_count)
    held = pair_owner[None, :] == slot_index[:, None]
    slot_first = jnp.sum(jnp.where(held, first_block[None, :], 0), axis=1)
    slot_second = jnp.sum(jnp.where(held, second_block[None, :], 0), axis=1)
    return (slot_first, slot_second)


def cross_terms(first_spec, second_spec):
    turned = jnp.stack([first_spec[:, :, :, 1], -first_spec[:, :, :, 0]], axis=3)
    real_part = jnp.einsum(
        "tispf,tjspf->itjf", first_spec, second_spec, preferred_element_type=jnp.float32
    )
    imag_part = jnp.einsum(
        "tispf,tjspf->itjf", turned, second_spec, preferred_element_type=jnp.float32
    )
    return jnp.stack([real_part, imag_part], axis=3).astype(jnp.bfloat16)


def invert(spectra, table, norm_factor):
    flat = spectra.reshape(-1, spectra.shape[3] * spectra.shape[4])
    lagged = jnp.dot(flat, table, preferred_element_type=jnp.float32) * norm_factor
    return lagged.reshape(spectra.shape[:3] + (table.shape[1],))


def on_device(traces, pair_offsets, pair_counts, pair_owner):
    block_size, local_segs, sample_count = traces.shape
    parts_count = lax.axis_size("seg")
    block_count = lax.axis_size("chan")
    quarter_bins = FREQS // parts_count
    all_segs = local_segs * parts_count
    norm_factor = 1.0 / math.sqrt(FREQS * all_segs)
    signal = traces.reshape(block_size * local_segs, sample_count)
    width_bins = min(128, FREQS)
    pieces_count = FREQS // width_bins
    times_axis = lax.iota(jnp.int32, sample_count)

    def transform(piece_index):
        bins_axis = BAND_START + piece_index * width_bins + lax.iota(jnp.int32, width_bins)
        phase_index = jnp.mod(times_axis[:, None] * bins_axis[None, :], sample_count)
        angles = phase_index.astype(jnp.float32) * (2.0 * math.pi / sample_count)
        table_part = jnp.concatenate([jnp.cos(angles), -jnp.sin(angles)], axis=1)
        table_high = table_part.astype(jnp.bfloat16)
        table_low = (table_part - table_high.astype(jnp.float32)).astype(jnp.bfloat16)
        upper = jnp.dot(signal, table_high, preferred_element_type=jnp.float32)
        return upper + jnp.dot(signal, table_low, preferred_element_type=jnp.float32)

    spectrum = lax.map(transform, lax.iota(jnp.int32, pieces_count))
    spectrum = (
        spectrum.reshape(pieces_count, -1, 2, width_bins)
        .transpose(1, 2, 0, 3)
        .reshape(-1, 2, FREQS)
    )
    real_part = spectrum[:, 0]
    imag_part = spectrum[:, 1]
    amplitude = jnp.sqrt(real_part * real_part + imag_part * imag_part)
    smoothed = jnp.dot(
        amplitude,
        smoother(FREQS),
        precision=lax.Precision.HIGHEST,
        preferred_element_type=jnp.float32,
    )
    divisor = jnp.maximum(smoothed, 1.0)
    whitened = jnp.stack([real_part / divisor, imag_part / divisor], axis=1).astype(jnp.bfloat16)
    whitened = whitened.reshape(block_size, local_segs, 2, parts_count, quarter_bins)
    quarter = lax.all_to_all(whitened, "seg", split_axis=3, concat_axis=1, tiled=True)
    quarter = quarter.reshape(block_size, all_segs, 2, quarter_bins)
    slot_first, slot_second = pair_blocks(
        pair_offsets, pair_counts, pair_owner, block_count, TILE_DEV * block_count
    )
    my_start = lax.axis_index("chan") * TILE_DEV
    needed = jnp.concatenate(
        [
            lax.dynamic_slice_in_dim(slot_first, my_start, TILE_DEV),
            lax.dynamic_slice_in_dim(slot_second, my_start, TILE_DEV),
        ]
    )
    empty_blocks = jnp.zeros((2 * TILE_DEV, block_size, all_segs, 2, quarter_bins), jnp.bfloat16)
    incoming = lax.all_gather(quarter, "chan", axis=0, tiled=True)
    block_total = incoming.shape[0] // block_size
    incoming_blocks = incoming.reshape(block_total, block_size, all_segs, 2, quarter_bins)
    inside = (needed >= 0) & (needed < block_total)
    picked = jnp.take(incoming_blocks, jnp.clip(needed, 0, block_total - 1), axis=0)
    held_blocks = jnp.where(inside[:, None, None, None, None], picked, empty_blocks)
    first_spec = held_blocks[:TILE_DEV]
    second_spec = held_blocks[TILE_DEV:]
    full_table = lag_table(0, FREQS)
    spectra = cross_terms(first_spec, second_spec)
    return invert(
        lax.all_to_all(spectra, "seg", split_axis=0, concat_axis=4, tiled=True),
        full_table,
        norm_factor,
    )


def solution(mesh):
    placed = (P("chan", "seg", None), P(), P(), P())
    return jax.shard_map(
        on_device,
        mesh=mesh,
        in_specs=placed,
        out_specs=P("seg", "chan", None, None),
        check_vma=False,
    )
```

profile of v0, /device:TPU:1, one launch (start us, length us, event | category | flops | bytes accessed | tf_op | source)
XLA Modules:
  0.0 643.9 jit_solution(6079321119400441198)
XLA Ops:
  6.5 0.1 convert_reduce_fusion
  6.6 7.2 %reshape.215 = bf16[256,8192]{1,0:T(8,128)(2,1)} reshape(bf16[128,2,8192]{2,1,0:T(2,128)(2,1)} %param.6) | data formatting | bytes 8388608 | tf_op jit(solution)/shard_map/reshape | solution.py:71
  13.8 82.4 %while.13 = (s32[]{:T(128)}, f32[4,256,256]{1,2,0:T(8,128)S(1)}, s32[4]{0:T(128)S(1)}, bf16[256,8192]{1,0:T(8,128)(2,1)}, s32[]{:T(128)}, /*index=5*/s32[1]{0:T(128)}, s32[1]{0:T(128)}) while((s32[]{:T(128)}, f32[4,256,256]{1,2,0:T(8,128)S(1)}, s32[4]{0:T(128)S(1)}, bf16[256,8192]{1,0:T(8,128)(2,1)}, s32[]{:T(128)}, ...), condition=%wide.region_8.9_spmd.clone, body=%wide.region_7.8_spmd.clone.sunk | while | flops 2182152192 | bytes 51119252 | solution.py:86
  13.8 0.7 dynamic_slice.19
  15.2 16.5 %fusion.57 = (f32[8192,128]{1,0:T(8,128)S(1)}, f32[8192,128]{1,0:T(8,128)S(1)}) fusion(s32[128]{0:T(128)S(1)} %iota_add_fusion.3), kind=kLoop, calls=%fused_computation.18.clone.1 | loop fusion | flops 15728640 | bytes 8389120 | tf_op jit(solution)/shard_map/while/body/eval_jaxpr/cos | solution.py:80
  31.7 1.3 fusion.58
  33.0 1.3 fusion.59
  34.4 0.7 dynamic_slice.19
  35.7 16.5 %fusion.57 = (f32[8192,128]{1,0:T(8,128)S(1)}, f32[8192,128]{1,0:T(8,128)S(1)}) fusion(s32[128]{0:T(128)S(1)} %iota_add_fusion.3), kind=kLoop, calls=%fused_computation.18.clone.1 | loop fusion | flops 15728640 | bytes 8389120 | tf_op jit(solution)/shard_map/while/body/eval_jaxpr/cos | solution.py:80
  52.3 1.3 fusion.58
  53.6 1.3 fusion.59
  54.9 0.7 dynamic_slice.19
  56.3 16.5 %fusion.57 = (f32[8192,128]{1,0:T(8,128)S(1)}, f32[8192,128]{1,0:T(8,128)S(1)}) fusion(s32[128]{0:T(128)S(1)} %iota_add_fusion.3), kind=kLoop, calls=%fused_computation.18.clone.1 | loop fusion | flops 15728640 | bytes 8389120 | tf_op jit(solution)/shard_map/while/body/eval_jaxpr/cos | solution.py:80
  72.8 1.3 fusion.58
  74.1 1.3 fusion.59
  75.5 0.7 dynamic_slice.19
  76.9 16.5 %fusion.57 = (f32[8192,128]{1,0:T(8,128)S(1)}, f32[8192,128]{1,0:T(8,128)S(1)}) fusion(s32[128]{0:T(128)S(1)} %iota_add_fusion.3), kind=kLoop, calls=%fused_computation.18.clone.1 | loop fusion | flops 15728640 | bytes 8389120 | tf_op jit(solution)/shard_map/while/body/eval_jaxpr/cos | solution.py:80
  93.4 1.3 fusion.58
  94.7 1.3 fusion.59
  96.2 0.4 copy.29
  96.6 0.4 reshape.217
  97.0 1.2 divide_convert_fusion.1
  98.6 15.9 %all_to_all.30 = bf16[128,2,2,4,128]{4,0,2,1,3:T(8,128)(2,1)} all-to-all(bf16[128,2,2,4,128]{4,0,2,1,3:T(8,128)(2,1)S(1)} %pad_maximum_fusion.2), channel_id=1, replica_groups=mesh['chan'=32,'seg'=4] {'seg'}, dimensions={3} | all-to-all | bytes 1048576 | tf_op jit(solution)/shard_map/all_to_all | solution.py:104
  114.5 0.1 copy.27
  114.6 0.1 reduce
  114.8 0.1 convert_reduce_fusion.1
  114.9 0.1 select_reduce_fusion.3
  115.0 0.1 select_reduce_fusion
  115.2 0.1 select_reduce_fusion.2
  115.3 0.1 dynamic_slice.13
  115.6 0.1 fusion.38
  115.7 0.1 compare_and_fusion.1
  115.8 186.4 %all-gather.2.cloned.1.call-done = bf16[4096,8,2,128]{3,0,2,1:T(8,128)(2,1)} async-done(((bf16[128,8,2,128]{3,0,2,1:T(8,128)(2,1)}), bf16[4096,8,2,128]{3,0,2,1:T(8,128)(2,1)}) %all-gather.2.cloned.1.call-update) | async-done | bytes 16777232 | tf_op jit(solution)/shard_map/all_gather | solution.py:117
  302.2 18.6 %copy.32 = bf16[4096,8,2,128]{3,1,2,0:T(8,128)(2,1)} copy(bf16[4096,8,2,128]{3,0,2,1:T(8,128)(2,1)} %all-gather.2.cloned.1.call-done) | data formatting | bytes 33554432 | tf_op jit(solution)/shard_map/all_gather | solution.py:117
  320.7 7.9 %gather_fusion = bf16[4,128,8,2,128]{4,2,3,1,0:T(8,128)(2,1)} fusion(bf16[32,128,8,2,128]{4,2,3,1,0:T(8,128)(2,1)} %bitcast.77, s32[1024]{0:T(1024)S(1)} %pad_clamp_fusion), kind=kCustom, calls=%fused_computation | custom fusion | bytes 4194320 | tf_op jit(solution)/shard_map/jit(_take)/gather | solution.py:121
  328.6 4.2 copy.33
  332.9 0.3 select_select_fusion
  333.2 0.1 fusion.42
  333.3 4.9 fusion.18
  338.2 4.9 fusion.19
  343.1 6.8 %pad_maximum_fusion.1 = bf16[128,2,128,2,128]{0,2,4,1,3:T(8,128)(2,1)} fusion(bf16[128,2,128,1,128]{0,2,4,1,3:T(8,128)(2,1)S(1)} %fusion.19, bf16[128,2,128,1,128]{0,2,4,1,3:T(8,128)(2,1)S(1)} %fusion.18), kind=kLoop, calls=%fused_computation.25 | loop fusion | flops 8388608 | bytes 33554432 | tf_op jit(solution)/shard_map/stack | solution.py:55
  349.9 23.5 %copy.34 = bf16[128,2,128,2,128]{2,4,1,3,0:T(8,128)(2,1)} copy(bf16[128,2,128,2,128]{0,2,4,1,3:T(8,128)(2,1)} %pad_maximum_fusion.1) | data formatting | bytes 33554432 | tf_op jit(solution)/shard_map/stack | solution.py:55
  373.4 12.9 %all-to-all-start.1 = ((bf16[128,2,128,2,128]{2,4,1,3,0:T(8,128)(2,1)}), bf16[128,2,128,2,128]{2,4,1,3,0:T(8,128)(2,1)}, u32[]{:S(2)}, u32[]{:S(2)}) async-start(bf16[128,2,128,2,128]{2,4,1,3,0:T(8,128)(2,1)} %copy.34), calls=%async_computation.1 | async-start | bytes 33554432 | tf_op jit(solution)/shard_map/all_to_all | solution.py:128
  386.3 2.5 cosine_convert_fusion
  388.8 181.2 %all-to-all-done.1 = bf16[128,2,128,2,128]{2,4,1,3,0:T(8,128)(2,1)} async-done(((bf16[128,2,128,2,128]{2,4,1,3,0:T(8,128)(2,1)}), bf16[128,2,128,2,128]{2,4,1,3,0:T(8,128)(2,1)}, u32[]{:S(2)}, u32[]{:S(2)}) %all-to-all-start.1) | async-done | bytes 16777248 | tf_op jit(solution)/shard_map/all_to_all | solution.py:128
  570.0 26.0 %copy.36 = bf16[32,2,128,2,4,128]{5,4,3,2,1,0:T(4,128)(2,1)} copy(bf16[32,2,128,2,4,128]{2,5,1,3,0,4:T(8,128)(2,1)} %bitcast.22) | data formatting | bytes 33554432 | tf_op jit(solution)/shard_map/all_to_all | solution.py:128
  596.0 27.3 %reshape.220 = bf16[8192,1024]{1,0:T(8,128)(2,1)} reshape(bf16[32,2,128,2,4,128]{5,4,3,2,1,0:T(4,128)(2,1)} %copy.36) | data formatting | bytes 33554432 | tf_op jit(solution)/shard_map/reshape | solution.py:59
  623.4 13.7 %convolution_multiply_fusion = f32[8192,256]{1,0:T(8,128)} fusion(bf16[8192,1024]{1,0:T(8,128)(2,1)} %reshape.220, bf16[512,256]{1,0:T(8,128)(2,1)S(1)} %get-tuple-element.99, bf16[512,256]{1,0:T(8,128)(2,1)S(1)} %get-tuple-element.98), kind=kOutput, calls=%fused_computation.28 | convolution fusion | flops 4298113024 | bytes 25690112 | tf_op jit(solution)/shard_map/dot_general | solution.py:60
  (41 shorter events, 0.8 us)
Async XLA Ops:
  6.5 295.6 %all-gather.2.cloned.1.call-start = ((), (), s32[]{:S(2)}) async-start(), calls=%async_computation.2 | async-start | bytes 17301504 | tf_op jit(solution)/shard_map/all_gather | solution.py:117
  15.2 16.5 %copy-start = (bf16[256,8192]{1,0:T(8,128)(2,1)S(1)}, bf16[256,8192]{1,0:T(8,128)(2,1)}, u32[]{:S(2)}) copy-start(bf16[256,8192]{1,0:T(8,128)(2,1)} %get-tuple-element.148) | copy-start | bytes 12582916 | tf_op jit(solution)/shard_map/while
  35.7 16.5 %copy-start = (bf16[256,8192]{1,0:T(8,128)(2,1)S(1)}, bf16[256,8192]{1,0:T(8,128)(2,1)}, u32[]{:S(2)}) copy-start(bf16[256,8192]{1,0:T(8,128)(2,1)} %get-tuple-element.148) | copy-start | bytes 12582916 | tf_op jit(solution)/shard_map/while
  56.3 16.5 %copy-start = (bf16[256,8192]{1,0:T(8,128)(2,1)S(1)}, bf16[256,8192]{1,0:T(8,128)(2,1)}, u32[]{:S(2)}) copy-start(bf16[256,8192]{1,0:T(8,128)(2,1)} %get-tuple-element.148) | copy-start | bytes 12582916 | tf_op jit(solution)/shard_map/while
  76.8 16.5 %copy-start = (bf16[256,8192]{1,0:T(8,128)(2,1)S(1)}, bf16[256,8192]{1,0:T(8,128)(2,1)}, u32[]{:S(2)}) copy-start(bf16[256,8192]{1,0:T(8,128)(2,1)} %get-tuple-element.148) | copy-start | bytes 12582916 | tf_op jit(solution)/shard_map/while
  98.2 16.2 %copy-start.2 = (s32[32]{0:T(128)S(1)}, s32[32]{0:T(128)}, u32[]{:S(2)}) copy-start(s32[32]{0:T(128)} %param.8) | copy-start | bytes 388
  98.2 16.5 %copy-start.1 = (s32[32,16]{0,1:T(8,128)S(1)}, s32[32,16]{0,1:T(8,128)}, u32[]{:S(2)}) copy-start(s32[32,16]{0,1:T(8,128)} %param.7) | copy-start | bytes 6148
  98.3 16.9 %copy-start.3 = (s32[64]{0:T(128)S(1)}, s32[64]{0:T(128)}, u32[]{:S(2)}) copy-start(s32[64]{0:T(128)} %param.9) | copy-start | bytes 772
  373.4 196.6 %all-to-all-start.1 = ((bf16[128,2,128,2,128]{2,4,1,3,0:T(8,128)(2,1)}), bf16[128,2,128,2,128]{2,4,1,3,0:T(8,128)(2,1)}, u32[]{:S(2)}, u32[]{:S(2)}) async-start(bf16[128,2,128,2,128]{2,4,1,3,0:T(8,128)(2,1)} %copy.34), calls=%async_computation.1 | async-start | bytes 33554432 | tf_op jit(solution)/shard_map/all_to_all | solution.py:128
Sparse Core Ops, SparseCore 0:
  114.6 187.5 all-gather.1
where the time goes:
time: 647 us; the launch traced here: 644 us
  waiting for transfers between devices  368 us (57%)
  local copies, waits for them, and re-layouts  119 us (18%)
  other arithmetic  76.8 us (12%)
  matrix products  35.1 us (5%)
  blocking collectives  15.9 us (2%)
  between operations  13.6 us (2%)
  starting transfers between devices  12.9 us (2%)
    all_gather x1, waiting for transfers between devices, on_device(): incoming = lax.all_gather(quarter, 'chan', axis=0, tiled=True)  186 us
    all_to_all x1, waiting for transfers between devices, on_device(): lax.all_to_all(spectra, 'seg', split_axis=0, concat_axis=4, tiled=True)  181 us
    cos x4, other arithmetic, transform(): table_part = jnp.concatenate([jnp.cos(angles), -jnp.sin(angles)], axis=1)  66.1 us
    reshape x1, local copies, waits for them, and re-layouts, invert(): flat = spectra.reshape(-1, spectra.shape[3] * spectra.shape[4])  27.3 us
    all_to_all x1, local copies, waits for them, and re-layouts, on_device(): lax.all_to_all(spectra, 'seg', split_axis=0, concat_axis=4, tiled=True)  26 us
    another operation x1, local copies, waits for them, and re-layouts, cross_terms(): return jnp.stack([real_part, imag_part], axis=3).astype(jnp.bfloat16)  23.5 us
    all_gather x1, local copies, waits for them, and re-layouts, on_device(): incoming = lax.all_gather(quarter, 'chan', axis=0, tiled=True)  18.6 us
    all_to_all x1, blocking collectives, on_device(): lax.all_to_all(whitened, 'seg', split_axis=3, concat_axis=1, tiled=True)  15.9 us
  transfers between devices with their start and end apart: 2, of which 2 were waited for; matrix products, arithmetic and copies ran while one was open for 1% of the time, Pallas kernels for 0%

commit v1 on v0

v1 whole, which is shorter than its diff:
```python
import math

import jax
import jax.numpy as jnp
import ml_dtypes
import numpy as np
from jax import lax
from jax.experimental import pallas as pl
from jax.experimental.pallas import tpu as pltpu
from jax.sharding import PartitionSpec as P

SAMPLES = 8192
BAND_START = 32
FREQS = 512
HALF = 8
LAGS = 256
BLOCK = 128
NBLK = 32
SEGS = 8
SLOT_DEV = 2
GROUP = 16
VMEM = 56 * 1024 * 1024


def dft_tables():
    phase = np.outer(np.arange(SAMPLES), BAND_START + np.arange(FREQS)) % SAMPLES
    ring = 2.0 * math.pi / SAMPLES * np.arange(SAMPLES)
    table = np.concatenate([np.cos(ring)[phase], -np.sin(ring)[phase]], axis=1)
    high = table.astype(np.float32).astype(ml_dtypes.bfloat16)
    low = (table - high.astype(np.float64)).astype(np.float32).astype(ml_dtypes.bfloat16)
    return high, low


def band_matrix():
    bins = np.arange(FREQS)
    near = np.abs(bins[:, None] - bins[None, :]) <= HALF
    return near.astype(ml_dtypes.bfloat16), near.sum(axis=0, keepdims=True).astype(np.float32)


def lag_tables():
    shifts = (np.arange(LAGS) - LAGS // 2) % SAMPLES
    phase = np.outer(BAND_START + np.arange(FREQS), shifts) % SAMPLES
    angles = phase.astype(np.float32) * np.float32(2.0 * math.pi / SAMPLES)
    norm = 1.0 / math.sqrt(FREQS * SEGS)
    parts = np.stack([np.cos(angles), -np.sin(angles)]).astype(ml_dtypes.bfloat16)
    parts = (parts.astype(np.float32) * norm).astype(ml_dtypes.bfloat16)
    parts = parts.reshape(2, FREQS // GROUP, 2, GROUP // 2, LAGS).transpose(4, 1, 0, 2, 3)
    both = np.stack([parts, parts[:, :, :, ::-1]])
    return both.reshape(2, LAGS, 2 * FREQS)


def group_mask():
    lane = np.arange(256)
    own = (lane // 16 % 2) * 8 + lane % 8
    return (np.arange(GROUP)[:, None] == own[None, :]).astype(np.float32)


def pair_blocks(pair_offsets, pair_counts, pair_owner, block_count, slot_count):
    slot_index = lax.iota(jnp.int32, slot_count)
    starts = jnp.cumsum(pair_counts) - pair_counts
    first_block = jnp.sum((starts[None, :] <= slot_index[:, None]).astype(jnp.int32), axis=1) - 1
    member = lax.iota(jnp.int32, block_count)[None, :] == first_block[:, None]
    start_of = jnp.sum(jnp.where(member, starts[None, :], 0), axis=1)
    position = slot_index - start_of
    listed = jnp.sum(jnp.where(member[:, :, None], pair_offsets[None, :, :], 0), axis=1)
    chosen = lax.iota(jnp.int32, pair_offsets.shape[1])[None, :] == position[:, None]
    offset = jnp.sum(jnp.where(chosen, listed, 0), axis=1)
    second_block = jnp.mod(first_block + offset, block_count)
    held = pair_owner[None, :] == slot_index[:, None]
    slot_first = jnp.sum(jnp.where(held, first_block[None, :], 0), axis=1)
    slot_second = jnp.sum(jnp.where(held, second_block[None, :], 0), axis=1)
    return (slot_first, slot_second)


def whiten_kernel(spec_ref, band_ref, count_ref, out_ref, tile_ref):
    band = band_ref[...]
    for tile in range(8):
        tile_ref[tile] = spec_ref[:, tile * BLOCK : (tile + 1) * BLOCK]
    turned = []
    for seg in range(2):
        rows = pl.ds(seg, BLOCK, stride=2)
        real = jnp.concatenate([tile_ref[tile, rows, :] for tile in range(4)], axis=1)
        imag = jnp.concatenate([tile_ref[tile, rows, :] for tile in range(4, 8)], axis=1)
        amplitude = jnp.sqrt(real * real + imag * imag)
        high = amplitude.astype(jnp.bfloat16)
        low = (amplitude - high.astype(jnp.float32)).astype(jnp.bfloat16)
        total = jnp.dot(high, band, preferred_element_type=jnp.float32)
        total = total + jnp.dot(low, band, preferred_element_type=jnp.float32)
        divisor = jnp.maximum(total / count_ref[...], 1.0)
        turned.append([(real / divisor).T, (imag / divisor).T])
    for part in range(2):
        pieces = [turned[seg][part].reshape(FREQS // 8, 1, 8, BLOCK) for seg in range(2)]
        both = jnp.concatenate(pieces, axis=1).reshape(NBLK, 2 * GROUP, BLOCK)
        out_ref[:, part * 2 * GROUP : (part + 1) * 2 * GROUP, :] = both.astype(jnp.bfloat16)


def select_kernel(first_ref, second_ref, place_ref, held_ref, out_ref, rows_ref):
    lane = lax.broadcasted_iota(jnp.int32, (32, BLOCK), 1)
    left = (lane < 64) == (place_ref[0] % 2 == 0)

    def turn(block, carry):
        tiles = held_ref[block].astype(jnp.float32)
        for core in range(2):
            order = tiles if core == 0 else jnp.concatenate(
                [tiles[16:32], tiles[0:16], tiles[48:64], tiles[32:48]], axis=0
            )
            twice = jnp.concatenate([order, order], axis=0)
            rows_ref[core, block] = twice.T.astype(jnp.bfloat16)
        return carry

    lax.fori_loop(0, NBLK, turn, 0)

    def send(chan, carry):
        slots = [SLOT_DEV * chan + slot for slot in range(SLOT_DEV)]
        for seg in range(4):
            core = seg % 2
            dest = 4 * chan + seg
            for slot in range(SLOT_DEV):
                second = second_ref[slots[slot]]
                for part in range(2):
                    out_ref[dest, pl.ds(32 * slot + 16 * part, 16), :] = held_ref[
                        second, pl.ds(32 * part + 16 * core, 16), :
                    ]
            one = rows_ref[core, first_ref[slots[0]], pl.ds(32 * seg, 32), :]
            two = rows_ref[core, first_ref[slots[1]], pl.ds(32 * seg, 32), :]
            out_ref[dest, pl.ds(64, 32), :] = jnp.where(left, one, two)
        return carry

    lax.fori_loop(0, NBLK, send, 0)


def correlate_kernel(core_ref, own_ref, other_ref, mask_ref, table_ref, out_ref, cross_ref):
    slot = pl.program_id(0)
    lane = lax.broadcasted_iota(jnp.int32, (32, BLOCK), 1)
    left = (lane < 64) == (slot == 0)

    def cross(group, carry):
        order = [slot, 1 - slot, 2 + slot, 3 - slot]
        upper = []
        lower = []
        for seg in order:
            src = 4 * group + seg
            tiles = []
            for part in range(2):
                rows = pl.ds(pl.multiple_of(32 * slot + 16 * part, 16), 16)
                tiles.append([own_ref[src, rows, :], other_ref[src, rows, :]])
            upper += tiles[0] + tiles[1]
            lower += [-tiles[1][0], -tiles[1][1], tiles[0][0], tiles[0][1]]
        second = jnp.concatenate(
            [jnp.concatenate(upper, axis=0), jnp.concatenate(lower, axis=0)], axis=1
        )
        lanes = [own_ref[4 * group + seg, pl.ds(64, 32), :] for seg in range(4)]
        first = jnp.concatenate(
            [jnp.where(left, lanes[0], lanes[1]), jnp.where(left, lanes[2], lanes[3])], axis=1
        ).astype(jnp.float32)
        mask = mask_ref[...]
        spread = [
            (jnp.broadcast_to(first[i : i + 1], (GROUP, 256)) * mask).astype(jnp.bfloat16)
            for i in range(32)
        ]
        found = jnp.dot(
            jnp.concatenate(spread, axis=0), second, preferred_element_type=jnp.float32
        ).astype(jnp.bfloat16)
        for part in range(2):
            cross_ref[:, 2 * group + part] = found[:, part * BLOCK : (part + 1) * BLOCK].reshape(
                32, GROUP, BLOCK
            )
        return carry

    lax.fori_loop(0, NBLK, cross, 0)

    def lags(pair, carry):
        sides = [cross_ref[2 * pair + k].reshape(2 * FREQS, BLOCK) for k in range(2)]
        lagged = jnp.dot(
            table_ref[0], jnp.concatenate(sides, axis=1), preferred_element_type=jnp.float32
        )
        for k in range(2):
            out_ref[2 * pair + k, 0] = lagged[:, k * BLOCK : (k + 1) * BLOCK].T
        return carry

    lax.fori_loop(0, 16, lags, 0)


def whiten(spectrum):
    band, count = band_matrix()
    return pl.pallas_call(
        whiten_kernel,
        out_shape=jax.ShapeDtypeStruct((NBLK, 4 * GROUP, BLOCK), jnp.bfloat16),
        scratch_shapes=[pltpu.VMEM((8, 2 * BLOCK, BLOCK), jnp.float32)],
        compiler_params=pltpu.CompilerParams(vmem_limit_bytes=VMEM),
        name="whiten",
    )(spectrum, jnp.asarray(band), jnp.asarray(count))


def select(slot_first, slot_second, place, held):
    smem = pl.BlockSpec(memory_space=pltpu.SMEM)
    return pl.pallas_call(
        select_kernel,
        out_shape=jax.ShapeDtypeStruct((128, 96, BLOCK), jnp.bfloat16),
        in_specs=[smem, smem, smem, pl.BlockSpec(memory_space=pltpu.VMEM)],
        scratch_shapes=[pltpu.VMEM((2, NBLK, BLOCK, BLOCK), jnp.bfloat16)],
        compiler_params=pltpu.CompilerParams(vmem_limit_bytes=VMEM),
        name="select",
    )(slot_first, slot_second, place, held)


def correlate(core, own, other):
    whole = lambda *shape: pl.BlockSpec(
        shape, lambda s, c: (0,) * len(shape), pipeline_mode=pl.Buffered(1)
    )
    return pl.pallas_call(
        correlate_kernel,
        out_shape=jax.ShapeDtypeStruct((32, SLOT_DEV, BLOCK, LAGS), jnp.float32),
        grid_spec=pltpu.PrefetchScalarGridSpec(
            num_scalar_prefetch=1,
            grid=(SLOT_DEV,),
            in_specs=[
                whole(128, 96, BLOCK),
                whole(128, 64, BLOCK),
                whole(GROUP, 256),
                pl.BlockSpec((1, LAGS, 2 * FREQS), lambda s, c: (c[0], 0, 0)),
            ],
            out_specs=pl.BlockSpec((32, 1, BLOCK, LAGS), lambda s, c: (0, s, 0, 0)),
            scratch_shapes=[pltpu.VMEM((32, 2 * FREQS // GROUP, GROUP, BLOCK), jnp.bfloat16)],
        ),
        compiler_params=pltpu.CompilerParams(vmem_limit_bytes=VMEM),
        name="correlate",
    )(core, own, other, jnp.asarray(group_mask()), jnp.asarray(lag_tables()))


def on_device(traces, pair_offsets, pair_counts, pair_owner):
    signal = traces.reshape(2 * BLOCK, SAMPLES)
    high, low = dft_tables()
    spectrum = jnp.dot(signal, jnp.asarray(high), preferred_element_type=jnp.float32)
    spectrum = spectrum + jnp.dot(signal, jnp.asarray(low), preferred_element_type=jnp.float32)
    slot_first, slot_second = pair_blocks(
        pair_offsets, pair_counts, pair_owner, NBLK, SLOT_DEV * NBLK
    )
    seg = lax.axis_index("seg").astype(jnp.int32).reshape(1)
    held = lax.all_to_all(whiten(spectrum), "chan", split_axis=0, concat_axis=0, tiled=True)
    sent = select(slot_first, slot_second, seg, held)
    own = lax.all_to_all(sent, ("chan", "seg"), split_axis=0, concat_axis=0, tiled=True)
    other = lax.ppermute(own[:, :64], "seg", [(0, 1), (1, 0), (2, 3), (3, 2)])
    return correlate(seg % 2, own, other)


def solution(mesh):
    placed = (P("chan", "seg", None), P(), P(), P())
    return jax.shard_map(
        on_device,
        mesh=mesh,
        in_specs=placed,
        out_specs=P("seg", "chan", None, None),
        check_vma=False,
    )
```

time: 647 us -> 145 us (0.22)
  waiting for transfers between devices: 368 us -> 12.5 us
  local copies, waits for them, and re-layouts: 119 us -> 13.4 us
  other arithmetic: 76.8 us -> 1.26 us
  Pallas kernels: 0 us -> 42.5 us
  blocking collectives: 15.9 us -> 50.3 us
  matrix products: 35.1 us -> 15 us
  between operations: 13.6 us -> 0.1 us
    all_gather x1 -> x0, waiting for transfers between devices: 186 us -> none  [on_device(): incoming = lax.all_gather(quarter, 'chan', axis=0, tiled=True)]
    all_to_all x1, waiting for transfers between devices: 181 us -> 8.33 us  [on_device(): lax.all_to_all(whiten(spectrum), 'chan', split_axis=0, concat_axis=0, til...]
    cos x4 -> x0, other arithmetic: 66.1 us -> none  [transform(): table_part = jnp.concatenate([jnp.cos(angles), -jnp.sin(angles)], axis=1)]
    pallas_call x0 -> x3, Pallas kernels: none -> 42.5 us  [the longest x1 32.9 us: correlate(): pl.pallas_call(correlate_kernel, out_shape=jax.ShapeDtypeStruct((32, SLOT...]
    all_to_all x1, blocking collectives: 15.9 us -> 50.3 us  [on_device(): lax.all_to_all(sent, ('chan', 'seg'), split_axis=0, concat_axis=0, tiled=...]
    reshape x4 -> x1, local copies, waits for them, and re-layouts: 35.3 us -> 7.17 us  [on_device(): signal = traces.reshape(2 * BLOCK, SAMPLES)]
    all_to_all x1 -> x0, local copies, waits for them, and re-layouts: 26 us -> none  [on_device(): lax.all_to_all(spectra, 'seg', split_axis=0, concat_axis=4, tiled=True)]
    another operation x6 -> x1, local copies, waits for them, and re-layouts: 23.8 us -> 0.09 us  [the longest x1 23.5 us: cross_terms(): return jnp.stack([real_part, imag_part], axis=3).astype(jnp.bfloat16)]
where the time goes in v1:
time: 145 us; the launch traced here: 144 us
  blocking collectives  50.3 us (35%)
  Pallas kernels  42.5 us (29%)
  matrix products  15 us (10%)
  local copies, waits for them, and re-layouts  13.4 us (9%)
  waiting for transfers between devices  12.5 us (9%)
  starting transfers between devices  9.31 us (6%)
    all_to_all x1, blocking collectives, on_device(): lax.all_to_all(sent, ('chan', 'seg'), split_axis=0, concat_axis=0, tiled=...  50.3 us
    pallas_call x1, Pallas kernels, correlate(): pl.pallas_call(correlate_kernel, out_shape=jax.ShapeDtypeStruct((32, SLOT...  32.9 us
    dot_general x1, matrix products, on_device(): jnp.dot(signal, jnp.asarray(high), preferred_element_type=jnp.float32)  9.45 us
    all_to_all x1, starting transfers between devices, on_device(): lax.all_to_all(whiten(spectrum), 'chan', split_axis=0, concat_axis=0, til...  9.22 us
    all_to_all x1, waiting for transfers between devices, on_device(): lax.all_to_all(whiten(spectrum), 'chan', split_axis=0, concat_axis=0, til...  8.33 us
    reshape x1, local copies, waits for them, and re-layouts, on_device(): signal = traces.reshape(2 * BLOCK, SAMPLES)  7.17 us
    pallas_call x1, Pallas kernels, select(): pl.pallas_call(select_kernel, out_shape=jax.ShapeDtypeStruct((128, 96, BL...  6.82 us
    unnamed x17, local copies, waits for them, and re-layouts  5.8 us
  transfers between devices with their start and end apart: 2, of which 2 were waited for; matrix products, arithmetic and copies ran while one was open for 1% of the time, Pallas kernels for 0%

profile of v1, /device:TPU:1, one launch (start us, length us, event | category | flops | bytes accessed | tf_op | source)
XLA Modules:
  0.0 144.3 jit_solution(5829145750598449277)
XLA Ops:
  0.0 7.2 %reshape.88 = bf16[256,8192]{1,0:T(8,128)(2,1)} reshape(bf16[128,2,8192]{2,1,0:T(2,128)(2,1)} %param.10) | data formatting | bytes 8388608 | tf_op jit(solution)/shard_map/reshape | solution.py:232
  7.2 0.0 copy-start.1
  7.2 0.0 copy-start.7
  7.2 9.5 %fusion.2 = f32[1024,256]{0,1:T(8,128)S(1)} fusion(bf16[256,8192]{1,0:T(8,128)(2,1)} %reshape.88, bf16[8192,1024]{1,0:T(8,128)(2,1)} %constant.57.clone), kind=kOutput, calls=%fused_computation.18 | convolution fusion | flops 4294967296 | bytes 22020096 | tf_op jit(solution)/shard_map/dot_general | solution.py:234
  16.6 0.0 copy-done.1
  16.6 3.5 %copy-done.7 = bf16[8192,1024]{1,0:T(8,128)(2,1)S(1)} copy-done((bf16[8192,1024]{1,0:T(8,128)(2,1)S(1)}, bf16[8192,1024]{1,0:T(8,128)(2,1)}, u32[]{:S(2)}) %copy-start.7) | copy-done | bytes 16777240
  20.2 0.0 copy-start.5
  20.2 0.0 copy-start.4
  20.2 0.0 copy-start.6
  20.2 5.6 %fusion.spec_ref = f32[256,1024]{1,0:T(8,128)} fusion(f32[1024,256]{0,1:T(8,128)S(1)} %fusion.2, bf16[256,8192]{1,0:T(8,128)(2,1)S(1)} %copy-done.1, bf16[8192,1024]{1,0:T(8,128)(2,1)S(1)} %copy-done.7), kind=kOutput, calls=%fused_computation.1 | convolution fusion | flops 4295229440 | bytes 23068672 | tf_op jit(solution)/shard_map/dot_general | solution.py:235
  25.7 2.8 %whiten.1 = bf16[32,64,128]{2,1,0:T(8,128)(2,1)} custom-call(f32[256,1024]{1,0:T(8,128)} %fusion.spec_ref, bf16[512,512]{1,0:T(8,128)(2,1)} %constant.59.clone.band_ref, f32[1,512]{1,0:T(1,128)} %constant.60.clone.count_ref), custom_call_target="tpu_custom_call" | custom-call | tf_op jit(solution)/shard_map/whiten/pallas_call | solution.py:186
  28.6 9.2 %all-to-all-start = ((bf16[32,64,128]{2,1,0:T(8,128)(2,1)}), bf16[32,64,128]{2,1,0:T(8,128)(2,1)S(1)}, u32[]{:S(2)}, u32[]{:S(2)}) async-start(bf16[32,64,128]{2,1,0:T(8,128)(2,1)} %whiten.1), calls=%async_computation | async-start | bytes 1048576 | tf_op jit(solution)/shard_map/all_to_all | solution.py:240
  37.8 0.0 copy-done.5
  37.8 0.1 copy.19
  37.9 0.1 reduce-window.9
  38.0 0.1 reduce
  38.1 0.1 convert_reduce_fusion
  38.2 0.1 select_reduce_fusion.3
  38.3 0.0 copy-done.4
  38.3 0.1 copy.20
  38.4 0.1 select_reduce_fusion
  38.6 0.0 copy-done.6
  38.6 0.7 select_reduce_fusion.1
  39.3 8.3 %all-to-all-done.held_ref = bf16[32,64,128]{2,1,0:T(8,128)(2,1)S(1)} async-done(((bf16[32,64,128]{2,1,0:T(8,128)(2,1)}), bf16[32,64,128]{2,1,0:T(8,128)(2,1)S(1)}, u32[]{:S(2)}, u32[]{:S(2)}) %all-to-all-start) | async-done | bytes 524320 | tf_op jit(solution)/shard_map/all_to_all | solution.py:240
  47.6 0.0 copy-start.3
  47.6 0.8 copy-done.3
  48.4 6.8 %select.11 = bf16[128,96,128]{2,1,0:T(8,128)(2,1)} custom-call(s32[64]{0:T(128)} %get-tuple-element.6.first_ref, s32[64]{0:T(128)} %get-tuple-element.5.second_ref, s32[1]{0:T(128)} %bitcast.place_ref, bf16[32,64,128]{2,1,0:T(8,128)(2,1)} %copy-done.3), custom_call_target="tpu_custom_call" | custom-call | tf_op jit(solution)/shard_map/select/pallas_call | solution.py:197
  55.2 50.3 %all_to_all.10.own_ref = bf16[128,96,128]{2,1,0:T(8,128)(2,1)S(1)} all-to-all(bf16[128,96,128]{2,1,0:T(8,128)(2,1)} %select.11), channel_id=1, replica_groups=mesh['chan'=32,'seg'=4] {'chan','seg'}, dimensions={0} | all-to-all | bytes 6291456 | tf_op jit(solution)/shard_map/all_to_all | solution.py:242
  105.5 0.0 copy-start
  105.5 0.3 slice.4
  105.9 0.1 collective-permute-start
  106.0 4.1 %collective-permute-done.other_ref = bf16[128,64,128]{2,1,0:T(8,128)(2,1)S(1)} collective-permute-done((bf16[128,64,128]{2,1,0:T(8,128)(2,1)S(1)}, bf16[128,64,128]{2,1,0:T(8,128)(2,1)S(1)}, u32[]{:S(2)}, u32[]{:S(2)}) %collective-permute-start) | collective-permute-done | bytes 2097184 | tf_op jit(solution)/shard_map/ppermute | solution.py:243
  110.1 0.0 copy-done
  110.1 0.0 copy-start.2
  110.1 1.4 copy-done.2
  111.5 32.9 %correlate.1 = f32[32,2,128,256]{3,2,1,0:T(8,128)} custom-call(s32[1]{0:T(128)S(6)} %select_n.36.core_ref, bf16[128,96,128]{2,1,0:T(8,128)(2,1)} %copy-done, bf16[128,64,128]{2,1,0:T(8,128)(2,1)} %copy-done.2, f32[16,256]{1,0:T(8,128)} %constant.61.clone.mask_ref, bf16[2,256,1024]{2,1,0:T(8,128)(2,1)} %constant.62.clone.table_ref), custom_call_target="tpu_custom_call" | custom-call | tf_op jit(solution)/shard_map/correlate/pallas_call | solution.py:211
  (6 shorter events, 0.1 us)
Async XLA Ops:
  7.2 9.5 %copy-start.1 = (bf16[256,8192]{1,0:T(8,128)(2,1)S(1)}, bf16[256,8192]{1,0:T(8,128)(2,1)}, u32[]{:S(2)}) copy-start(bf16[256,8192]{1,0:T(8,128)(2,1)} %reshape.88) | copy-start | bytes 12582916
  7.2 13.0 %copy-start.7 = (bf16[8192,1024]{1,0:T(8,128)(2,1)S(1)}, bf16[8192,1024]{1,0:T(8,128)(2,1)}, u32[]{:S(2)}) copy-start(bf16[8192,1024]{1,0:T(8,128)(2,1)} %constant.58.clone) | copy-start | bytes 50331652
  20.2 17.6 %copy-start.5 = (s32[32]{0:T(128)S(1)}, s32[32]{0:T(128)}, u32[]{:S(2)}) copy-start(s32[32]{0:T(128)} %param.12) | copy-start | bytes 388
  20.2 18.1 %copy-start.4 = (s32[32,16]{0,1:T(8,128)S(1)}, s32[32,16]{0,1:T(8,128)}, u32[]{:S(2)}) copy-start(s32[32,16]{0,1:T(8,128)} %param.11) | copy-start | bytes 6148
  20.2 18.4 %copy-start.6 = (s32[64]{0:T(128)S(1)}, s32[64]{0:T(128)}, u32[]{:S(2)}) copy-start(s32[64]{0:T(128)} %param.13) | copy-start | bytes 772
  28.6 19.0 %all-to-all-start = ((bf16[32,64,128]{2,1,0:T(8,128)(2,1)}), bf16[32,64,128]{2,1,0:T(8,128)(2,1)S(1)}, u32[]{:S(2)}, u32[]{:S(2)}) async-start(bf16[32,64,128]{2,1,0:T(8,128)(2,1)} %whiten.1), calls=%async_computation | async-start | bytes 1048576 | tf_op jit(solution)/shard_map/all_to_all | solution.py:240
  47.6 0.8 copy-start.3
  105.5 4.6 %copy-start = (bf16[128,96,128]{2,1,0:T(8,128)(2,1)}, bf16[128,96,128]{2,1,0:T(8,128)(2,1)S(1)}, u32[]{:S(2)}) copy-start(bf16[128,96,128]{2,1,0:T(8,128)(2,1)S(1)} %all_to_all.10.own_ref) | copy-start | bytes 9437188
  105.9 4.2 %collective-permute-start = (bf16[128,64,128]{2,1,0:T(8,128)(2,1)S(1)}, bf16[128,64,128]{2,1,0:T(8,128)(2,1)S(1)}, u32[]{:S(2)}, u32[]{:S(2)}) collective-permute-start(bf16[128,64,128]{2,1,0:T(8,128)(2,1)S(1)} %slice.4), channel_id=1, source_target_pairs={{0,1},{1,0},{2,3},{3,2},{4,5},{5,4},{6,7},{7,6},{8,9},{9,8},{10,11... | collective-permute-start | bytes 6291464 | tf_op jit(solution)/shard_map/ppermute | solution.py:243
  110.1 1.4 copy-start.2

commit v2 on v1

v2 whole, which is shorter than its diff:
```python
import math

import jax
import jax.numpy as jnp
import ml_dtypes
import numpy as np
from jax import lax
from jax.experimental import pallas as pl
from jax.experimental.pallas import tpu as pltpu
from jax.sharding import PartitionSpec as P

SAMPLES = 8192
BAND_START = 32
FREQS = 512
HALF = 8
LAGS = 256
BLOCK = 128
NBLK = 32
SEGS = 8
SLOT_DEV = 2
GROUP = 16
RADIX = 16
VMEM = 32 * 1024 * 1024
PAIRS = 4
UNROLL = 32
FETCHES = 8


def bin_order():
    residues = [(0, 8)] + [(unit, RADIX - unit) for unit in range(1, RADIX // 2)]
    return (np.array(residues)[:, :, None] + RADIX * np.arange(FREQS // RADIX)).reshape(-1)


def dft_tables():
    run = SAMPLES // RADIX
    ring = 2.0 * math.pi / SAMPLES * np.arange(SAMPLES)
    bins = bin_order().reshape(RADIX // 2, 2, FREQS // RADIX)
    table = np.zeros((RADIX // 2, 2, run, 2, 2, FREQS // RADIX))
    for unit in range(RADIX // 2):
        for side in range(2):
            phase = np.outer(np.arange(run), BAND_START + bins[unit, side]) % SAMPLES
            cosine, sine = np.cos(ring)[phase], np.sin(ring)[phase]
            if unit == 0:
                table[unit, side, :, 0, side] = cosine
                table[unit, side, :, 1, side] = -sine
            else:
                sign = 1.0 if side == 0 else -1.0
                table[unit, 0, :, 0, side] = cosine
                table[unit, 0, :, 1, side] = -sine
                table[unit, 1, :, 0, side] = -sign * sine
                table[unit, 1, :, 1, side] = -sign * cosine
    table = table.reshape(RADIX // 2, 2 * run, BLOCK)
    high = table.astype(np.float32).astype(ml_dtypes.bfloat16)
    low = (table - high.astype(np.float64)).astype(np.float32).astype(ml_dtypes.bfloat16)
    return np.concatenate([high, low], axis=2)


def band_tables():
    bins = bin_order()
    near = np.abs(bins[:, None] - bins[None, :]) <= HALF
    order = np.arange(FREQS)[:, None] == bins[None, :]
    return (
        near.astype(ml_dtypes.bfloat16),
        order.astype(ml_dtypes.bfloat16),
    )


def lag_tables():
    shifts = (np.arange(LAGS) - LAGS // 2) % SAMPLES
    phase = np.outer(BAND_START + np.arange(FREQS), shifts) % SAMPLES
    angles = phase.astype(np.float32) * np.float32(2.0 * math.pi / SAMPLES)
    norm = 1.0 / math.sqrt(FREQS * SEGS)
    parts = np.stack([np.cos(angles), -np.sin(angles)]).astype(ml_dtypes.bfloat16)
    parts = (parts.astype(np.float32) * norm).astype(ml_dtypes.bfloat16)
    parts = parts.reshape(2, FREQS // GROUP, 2, GROUP // 2, LAGS).transpose(4, 1, 0, 2, 3)
    both = np.stack([parts, parts[:, :, :, ::-1]])
    return both.reshape(2, LAGS, 2 * FREQS)


def group_mask():
    lane = np.arange(256)
    own = (lane // 16 % 2) * 8 + lane % 8
    return (np.arange(GROUP)[:, None] == own[None, :]).astype(ml_dtypes.bfloat16)


def pair_blocks(pair_offsets, pair_counts, pair_owner, block_count, slot_count):
    slot_index = lax.iota(jnp.int32, slot_count)
    starts = jnp.cumsum(pair_counts) - pair_counts
    first_block = jnp.sum((starts[None, :] <= slot_index[:, None]).astype(jnp.int32), axis=1) - 1
    member = lax.iota(jnp.int32, block_count)[None, :] == first_block[:, None]
    start_of = jnp.sum(jnp.where(member, starts[None, :], 0), axis=1)
    position = slot_index - start_of
    listed = jnp.sum(jnp.where(member[:, :, None], pair_offsets[None, :, :], 0), axis=1)
    chosen = lax.iota(jnp.int32, pair_offsets.shape[1])[None, :] == position[:, None]
    offset = jnp.sum(jnp.where(chosen, listed, 0), axis=1)
    second_block = jnp.mod(first_block + offset, block_count)
    held = pair_owner[None, :] == slot_index[:, None]
    slot_first = jnp.sum(jnp.where(held, first_block[None, :], 0), axis=1)
    slot_second = jnp.sum(jnp.where(held, second_block[None, :], 0), axis=1)
    return (slot_first, slot_second)


def butterflies(x):
    root, c1, c3 = math.sqrt(0.5), math.cos(math.pi / 8), math.cos(3 * math.pi / 8)
    a = [x[n] + x[n + 8] for n in range(8)]
    b = [x[n] - x[n + 8] for n in range(8)]
    c = [a[n] + a[n + 4] for n in range(4)]
    d = [a[n] - a[n + 4] for n in range(4)]
    even, odd = c[0] + c[2], c[1] + c[3]
    g, h = (d[1] - d[3]) * root, (d[1] + d[3]) * root
    p = [None] + [b[n] - b[8 - n] for n in range(1, 4)]
    q = [None] + [b[n] + b[8 - n] for n in range(1, 4)]
    p2, q2 = p[2] * root, q[2] * root
    re1, re3 = p[1] * c1 + p[3] * c3, p[1] * c3 - p[3] * c1
    im1, im3 = q[1] * c3 + q[3] * c1, q[1] * c1 - q[3] * c3
    plus, minus = b[0] + p2, b[0] - p2
    over, under = q2 + b[4], q2 - b[4]
    return [
        (even + odd, even - odd),
        (plus + re1, im1 + over),
        (d[0] + g, d[2] + h),
        (minus + re3, im3 + under),
        (c[0] - c[2], c[1] - c[3]),
        (minus - re3, im3 - under),
        (d[0] - g, h - d[2]),
        (plus - re1, im1 - over),
    ]


def front_kernel(
    rows_hbm, dft_hbm, band_hbm, order_hbm, out_ref,
    rows_ref, dft_ref, band_ref, order_ref, sums_ref, row_sem, table_sem,
):
    each = BLOCK * BLOCK // FETCHES
    copies = []
    for fetch in range(FETCHES):
        part = pl.ds(each * fetch, each)
        copies.append(
            pltpu.make_async_copy(rows_hbm.at[part], rows_ref.at[part], row_sem.at[fetch])
        )
        copies[fetch].start()
    fetched = [(dft_hbm, dft_ref), (band_hbm, band_ref), (order_hbm, order_ref)]
    tables = [
        pltpu.make_async_copy(source, target, table_sem.at[which])
        for which, (source, target) in enumerate(fetched)
    ]
    for table in tables:
        table.start()

    def channel(chan, carry):
        x = []
        for pair in range(RADIX // 2):
            tile = rows_ref[pl.ds(pl.multiple_of(BLOCK * chan + 16 * pair, 16), 16), :]
            tile = tile.astype(jnp.float32)
            x += [tile[:8], tile[8:]]
        for unit, sums in enumerate(butterflies(x)):
            for side in range(2):
                sums_ref[2 * unit + side, pl.ds(pl.multiple_of(8 * chan, 8), 8), :] = sums[side]
        return carry

    for fetch in range(FETCHES):
        copies[fetch].wait()
        count = BLOCK // FETCHES
        lax.fori_loop(count * fetch, count * (fetch + 1), channel, 0, unroll=4)

    for table in tables:
        table.wait()
    found = []
    for unit in range(RADIX // 2):
        columns = []
        for side in range(2):
            for tile in range(4):
                part = [
                    sums_ref[2 * unit + side, pl.ds(2 * tile + seg, BLOCK, stride=8), :]
                    for seg in range(2)
                ]
                columns.append(jnp.concatenate(part, axis=0))
        exact = jnp.concatenate(columns, axis=1)
        high = exact.astype(jnp.bfloat16)
        low = (exact - high.astype(jnp.float32)).astype(jnp.bfloat16)
        first = jnp.dot(high, dft_ref[unit], preferred_element_type=jnp.float32)
        rest = jnp.dot(low, dft_ref[unit, :, :BLOCK], preferred_element_type=jnp.float32)
        found.append(first[:, :BLOCK] + (first[:, BLOCK:] + rest))
    left = lax.broadcasted_iota(jnp.int32, (2 * BLOCK, BLOCK), 1) < 64
    real = []
    imag = []
    for one, two in zip(found[0::2], found[1::2]):
        real.append(jnp.where(left, one, pltpu.roll(two, 64, 1)))
        imag.append(jnp.where(left, pltpu.roll(one, 64, 1), two))
    real = jnp.concatenate(real, axis=1)
    imag = jnp.concatenate(imag, axis=1)
    amplitude = jnp.sqrt(real * real + imag * imag)
    high = amplitude.astype(jnp.bfloat16)
    low = (amplitude - high.astype(jnp.float32)).astype(jnp.bfloat16)
    band = band_ref[...]
    total = jnp.dot(high, band, preferred_element_type=jnp.float32)
    total = total + jnp.dot(low, band, preferred_element_type=jnp.float32)
    count = jnp.dot(jnp.ones((8, FREQS), jnp.bfloat16), band, preferred_element_type=jnp.float32)
    divisor = jnp.maximum(total / count[:1], 1.0)
    for part, spectrum in enumerate([real, imag]):
        white = (spectrum / divisor).astype(jnp.bfloat16)
        turned = lax.dot_general(
            order_ref[...], white, (((1,), (1,)), ((), ())), preferred_element_type=jnp.float32
        )
        pieces = [
            turned[:, BLOCK * seg : BLOCK * (seg + 1)].reshape(FREQS // 8, 1, 8, BLOCK)
            for seg in range(2)
        ]
        both = jnp.concatenate(pieces, axis=1).reshape(NBLK, 2 * GROUP, BLOCK)
        out_ref[:, part * 2 * GROUP : (part + 1) * 2 * GROUP, :] = both.astype(jnp.bfloat16)


def select_kernel(first_ref, second_ref, place_ref, held_ref, out_ref, rows_ref):
    lane = lax.broadcasted_iota(jnp.int32, (32, BLOCK), 1)
    left = (lane < 64) == (place_ref[0] % 2 == 0)

    def turn(block, carry):
        tiles = held_ref[block].astype(jnp.float32)
        for core in range(2):
            order = tiles if core == 0 else jnp.concatenate(
                [tiles[16:32], tiles[0:16], tiles[48:64], tiles[32:48]], axis=0
            )
            twice = jnp.concatenate([order, order], axis=0)
            rows_ref[core, block] = twice.T.astype(jnp.bfloat16)
        return carry

    lax.fori_loop(0, NBLK, turn, 0)

    def send(chan, carry):
        slots = [SLOT_DEV * chan + slot for slot in range(SLOT_DEV)]
        for seg in range(4):
            core = seg % 2
            dest = 4 * chan + seg
            for slot in range(SLOT_DEV):
                second = second_ref[slots[slot]]
                for part in range(2):
                    out_ref[dest, pl.ds(32 * slot + 16 * part, 16), :] = held_ref[
                        second, pl.ds(32 * part + 16 * core, 16), :
                    ]
            one = rows_ref[core, first_ref[slots[0]], pl.ds(32 * seg, 32), :]
            two = rows_ref[core, first_ref[slots[1]], pl.ds(32 * seg, 32), :]
            out_ref[dest, pl.ds(64, 32), :] = jnp.where(left, one, two)
        return carry

    lax.fori_loop(0, NBLK, send, 0)


def correlate_kernel(
    core_ref, own_ref, other_ref, mask_ref, table_ref, out_hbm, cross_ref, lag_ref, out_sem
):
    core = core_ref[0]
    leaving = []
    for slot in range(SLOT_DEV):

        def cross(group, carry):
            order = [slot, 1 - slot, 2 + slot, 3 - slot]
            upper = []
            lower = []
            for seg in order:
                src = 4 * group + seg
                tiles = []
                for part in range(2):
                    rows = pl.ds(32 * slot + 16 * part, 16)
                    tiles.append([own_ref[src, rows, :], other_ref[src, rows, :]])
                upper += tiles[0] + tiles[1]
                lower += [-tiles[1][0], -tiles[1][1]] + tiles[0]
            second = jnp.concatenate(
                [jnp.concatenate(upper, axis=0), jnp.concatenate(lower, axis=0)], axis=1
            )
            lane = lax.broadcasted_iota(jnp.int32, (32, BLOCK), 1)
            left = (lane < 64) == (slot == 0)
            lanes = [own_ref[4 * group + seg, pl.ds(64, 32), :] for seg in range(4)]
            first = jnp.concatenate(
                [jnp.where(left, lanes[0], lanes[1]), jnp.where(left, lanes[2], lanes[3])], axis=1
            )
            mask = mask_ref[...]
            spread = [jnp.broadcast_to(first[i : i + 1], (GROUP, 256)) * mask for i in range(32)]
            found = jnp.dot(
                jnp.concatenate(spread, axis=0), second, preferred_element_type=jnp.float32
            ).astype(jnp.bfloat16)
            for part in range(2):
                cross_ref[:, 2 * group + part] = found[
                    :, part * BLOCK : (part + 1) * BLOCK
                ].reshape(32, GROUP, BLOCK)
            return carry

        def lags(pair, carry):
            sides = [cross_ref[2 * pair + k].reshape(2 * FREQS, BLOCK) for k in range(2)]
            lagged = jnp.dot(
                table_ref[core], jnp.concatenate(sides, axis=1), preferred_element_type=jnp.float32
            )
            for k in range(2):
                lag_ref[slot, 2 * pair + k] = lagged[:, k * BLOCK : (k + 1) * BLOCK].T
            return carry

        lax.fori_loop(0, NBLK, cross, 0, unroll=UNROLL)
        for step in range(16 // PAIRS):
            lax.fori_loop(PAIRS * step, PAIRS * (step + 1), lags, 0, unroll=True)
            rows = pl.ds(2 * PAIRS * step, 2 * PAIRS)
            copy = pltpu.make_async_copy(
                lag_ref.at[slot, rows], out_hbm.at[rows, slot], out_sem.at[slot, step]
            )
            copy.start()
            leaving.append(copy)
    for copy in leaving:
        copy.wait()


def front(traces):
    band, order = band_tables()
    rows = traces.reshape(BLOCK, 2, SAMPLES // BLOCK, BLOCK).transpose(0, 2, 1, 3)
    rows = rows.reshape(BLOCK * BLOCK, BLOCK)
    vmem = pl.BlockSpec(memory_space=pltpu.VMEM)
    return pl.pallas_call(
        front_kernel,
        out_shape=jax.ShapeDtypeStruct((NBLK, 4 * GROUP, BLOCK), jnp.bfloat16),
        in_specs=[pl.BlockSpec(memory_space=pltpu.HBM)] * 4,
        out_specs=vmem,
        scratch_shapes=[
            pltpu.VMEM((BLOCK * BLOCK, BLOCK), jnp.bfloat16),
            pltpu.VMEM((RADIX // 2, 1024, 2 * BLOCK), jnp.bfloat16),
            pltpu.VMEM((FREQS, FREQS), jnp.bfloat16),
            pltpu.VMEM((FREQS, FREQS), jnp.bfloat16),
            pltpu.VMEM((RADIX, 8 * BLOCK, BLOCK), jnp.float32),
            pltpu.SemaphoreType.DMA((FETCHES,)),
            pltpu.SemaphoreType.DMA((3,)),
        ],
        compiler_params=pltpu.CompilerParams(vmem_limit_bytes=VMEM),
        name="front",
    )(
        *[pltpu.with_memory_space_constraint(jnp.asarray(each), pltpu.HBM)
          for each in (rows, dft_tables(), band, order)]
    )


def select(slot_first, slot_second, place, held):
    smem = pl.BlockSpec(memory_space=pltpu.SMEM)
    return pl.pallas_call(
        select_kernel,
        out_shape=jax.ShapeDtypeStruct((128, 96, BLOCK), jnp.bfloat16),
        in_specs=[smem, smem, smem, pl.BlockSpec(memory_space=pltpu.VMEM)],
        scratch_shapes=[pltpu.VMEM((2, NBLK, BLOCK, BLOCK), jnp.bfloat16)],
        compiler_params=pltpu.CompilerParams(vmem_limit_bytes=VMEM),
        name="select",
    )(slot_first, slot_second, place, held)


def correlate(core, own, other):
    vmem = pl.BlockSpec(memory_space=pltpu.VMEM)
    return pl.pallas_call(
        correlate_kernel,
        out_shape=jax.ShapeDtypeStruct((32, SLOT_DEV, BLOCK, LAGS), jnp.float32),
        in_specs=[pl.BlockSpec(memory_space=pltpu.SMEM), vmem, vmem, vmem, vmem],
        out_specs=pl.BlockSpec(memory_space=pl.ANY),
        scratch_shapes=[
            pltpu.VMEM((32, 2 * FREQS // GROUP, GROUP, BLOCK), jnp.bfloat16),
            pltpu.VMEM((SLOT_DEV, 32, BLOCK, LAGS), jnp.float32),
            pltpu.SemaphoreType.DMA((SLOT_DEV, 16 // PAIRS)),
        ],
        compiler_params=pltpu.CompilerParams(vmem_limit_bytes=VMEM),
        name="correlate",
    )(core, own, other, jnp.asarray(group_mask()), jnp.asarray(lag_tables()))


def on_device(traces, pair_offsets, pair_counts, pair_owner):
    slot_first, slot_second = pair_blocks(
        pair_offsets, pair_counts, pair_owner, NBLK, SLOT_DEV * NBLK
    )
    seg = lax.axis_index("seg").astype(jnp.int32).reshape(1)
    held = lax.all_to_all(front(traces), "chan", split_axis=0, concat_axis=0, tiled=True)
    sent = select(slot_first, slot_second, seg, held)
    own = lax.all_to_all(sent, ("chan", "seg"), split_axis=0, concat_axis=0, tiled=True)
    other = lax.ppermute(own[:, :64], "seg", [(0, 1), (1, 0), (2, 3), (3, 2)])
    return correlate(seg % 2, own, other)


def solution(mesh):
    placed = (P("chan", "seg", None), P(), P(), P())
    return jax.shard_map(
        on_device,
        mesh=mesh,
        in_specs=placed,
        out_specs=P("seg", "chan", None, None),
        check_vma=False,
    )
```

time: 145 us -> 97.6 us (0.67)
  Pallas kernels: 42.5 us -> 23.3 us
  matrix products: 15 us -> 0 us
  local copies, waits for them, and re-layouts: 13.4 us -> 0.49 us
    pallas_call x1, Pallas kernels: 32.9 us -> 10.6 us  [correlate(): pl.pallas_call(correlate_kernel, out_shape=jax.ShapeDtypeStruct((32, SLOT...]
    dot_general x2 -> x0, matrix products: 15 us -> none  [the longest x1 9.45 us: on_device(): jnp.dot(signal, jnp.asarray(high), preferred_element_type=jnp.float32)]
    reshape x1 -> x0, local copies, waits for them, and re-layouts: 7.17 us -> none  [on_device(): signal = traces.reshape(2 * BLOCK, SAMPLES)]
    unnamed x17 -> x11, local copies, waits for them, and re-layouts: 5.8 us -> 0.09 us
    pallas_call x1, Pallas kernels: 2.83 us -> 8.04 us  [front(): pl.pallas_call(front_kernel, out_shape=jax.ShapeDtypeStruct((NBLK, 4 * GR...]
    pallas_call x1, Pallas kernels: 6.82 us -> 4.65 us  [select(): pl.pallas_call(select_kernel, out_shape=jax.ShapeDtypeStruct((128, 96, BL...]
where the time goes in v2:
time: 97.6 us; the launch traced here: 97.4 us
  blocking collectives  50.1 us (51%)
  Pallas kernels  23.3 us (24%)
  waiting for transfers between devices  13.1 us (13%)
  starting transfers between devices  9.5 us (10%)
    all_to_all x1, blocking collectives, on_device(): lax.all_to_all(sent, ('chan', 'seg'), split_axis=0, concat_axis=0, tiled=...  50.1 us
    pallas_call x1, Pallas kernels, correlate(): pl.pallas_call(correlate_kernel, out_shape=jax.ShapeDtypeStruct((32, SLOT...  10.6 us
    all_to_all x1, starting transfers between devices, on_device(): lax.all_to_all(front(traces), 'chan', split_axis=0, concat_axis=0, tiled=...  9.24 us
    all_to_all x1, waiting for transfers between devices, on_device(): lax.all_to_all(front(traces), 'chan', split_axis=0, concat_axis=0, tiled=...  8.92 us
    pallas_call x1, Pallas kernels, front(): pl.pallas_call(front_kernel, out_shape=jax.ShapeDtypeStruct((NBLK, 4 * GR...  8.04 us
    pallas_call x1, Pallas kernels, select(): pl.pallas_call(select_kernel, out_shape=jax.ShapeDtypeStruct((128, 96, BL...  4.65 us
    ppermute x1, waiting for transfers between devices, on_device(): other = lax.ppermute(own[:, :64], 'seg', [(0, 1), (1, 0), (2, 3), (3, 2)])  4.14 us
  transfers between devices with their start and end apart: 2, of which 2 were waited for; matrix products, arithmetic and copies ran while one was open for 1% of the time, Pallas kernels for 0%

profile of v2, /device:TPU:1, one launch (start us, length us, event | category | flops | bytes accessed | tf_op | source)
XLA Modules:
  0.0 97.4 jit_solution(2910195262113215498)
XLA Ops:
  0.0 0.0 copy-start.3
  0.0 0.0 copy-start.2
  0.0 0.0 copy-start.4
  0.0 8.0 %front.1 = bf16[32,64,128]{2,1,0:T(8,128)(2,1)} custom-call(bf16[16384,128]{1,0:T(8,128)(2,1)} %bitcast.7, bf16[8,1024,256]{2,1,0:T(8,128)(2,1)} %constant.55.clone.dft_hbm, bf16[512,512]{1,0:T(8,128)(2,1)} %constant.56.clone.band_hbm, bf16[512,512]{1,0:T(8,128)(2,1)} %constant.57.clone.order_hbm), custom_call_target="tpu_custom_call" | custom-call | tf_op jit(solution)/shard_map/front/pallas_call | solution.py:314
  8.1 9.2 %all-to-all-start = ((bf16[32,64,128]{2,1,0:T(8,128)(2,1)}), bf16[32,64,128]{2,1,0:T(8,128)(2,1)S(1)}, u32[]{:S(2)}, u32[]{:S(2)}) async-start(bf16[32,64,128]{2,1,0:T(8,128)(2,1)} %front.1), calls=%async_computation | async-start | bytes 1048576 | tf_op jit(solution)/shard_map/all_to_all | solution.py:370
  17.3 0.0 copy-done.3
  17.3 0.1 copy.16
  17.4 0.1 reduce-window.9
  17.5 0.1 reduce
  17.6 0.1 convert_reduce_fusion
  17.7 0.1 select_reduce_fusion.3
  17.8 0.0 copy-done.2
  17.8 0.1 copy.17
  17.9 0.1 select_reduce_fusion
  18.1 0.0 copy-done.4
  18.1 0.1 select_reduce_fusion.1
  18.2 8.9 %all-to-all-done.held_ref = bf16[32,64,128]{2,1,0:T(8,128)(2,1)S(1)} async-done(((bf16[32,64,128]{2,1,0:T(8,128)(2,1)}), bf16[32,64,128]{2,1,0:T(8,128)(2,1)S(1)}, u32[]{:S(2)}, u32[]{:S(2)}) %all-to-all-start) | async-done | bytes 524320 | tf_op jit(solution)/shard_map/all_to_all | solution.py:370
  27.1 4.7 %select.11 = bf16[128,96,128]{2,1,0:T(8,128)(2,1)S(1)} custom-call(s32[64]{0:T(128)S(1)} %get-tuple-element.6.first_ref, s32[64]{0:T(128)S(1)} %get-tuple-element.5.second_ref, s32[1]{0:T(128)} %bitcast.place_ref, bf16[32,64,128]{2,1,0:T(8,128)(2,1)S(1)} %all-to-all-done.held_ref), custom_call_target="tpu_custom_call" | custom-call | tf_op jit(solution)/shard_map/select/pallas_call | solution.py:338
  31.8 50.1 %all_to_all.10.own_ref = bf16[128,96,128]{2,1,0:T(8,128)(2,1)S(1)} all-to-all(bf16[128,96,128]{2,1,0:T(8,128)(2,1)S(1)} %select.11), channel_id=1, replica_groups=mesh['chan'=32,'seg'=4] {'chan','seg'}, dimensions={0} | all-to-all | bytes 6291456 | tf_op jit(solution)/shard_map/all_to_all | solution.py:372
  81.9 0.0 copy-start
  81.9 0.0 copy-start.1
  81.9 0.3 slice.4
  82.2 0.3 collective-permute-start
  82.5 4.1 %collective-permute-done.other_ref = bf16[128,64,128]{2,1,0:T(8,128)(2,1)S(1)} collective-permute-done((bf16[128,64,128]{2,1,0:T(8,128)(2,1)S(1)}, bf16[128,64,128]{2,1,0:T(8,128)(2,1)S(1)}, u32[]{:S(2)}, u32[]{:S(2)}) %collective-permute-start) | collective-permute-done | bytes 2097184 | tf_op jit(solution)/shard_map/ppermute | solution.py:373
  86.6 0.0 copy-done
  86.6 0.0 copy-done.1
  86.6 10.6 %correlate.1 = f32[32,2,128,256]{3,2,1,0:T(8,128)} custom-call(s32[1]{0:T(128)S(6)} %select_n.36.core_ref, bf16[128,96,128]{2,1,0:T(8,128)(2,1)S(1)} %all_to_all.10.own_ref, bf16[128,64,128]{2,1,0:T(8,128)(2,1)S(1)} %collective-permute-done.other_ref, bf16[16,256]{1,0:T(8,128)(2,1)S(1)} %copy-done.1, bf16[2,256,1024]{2,1,0:T(8,128)(2,1)S(1)} %copy-done), custom_call_target="tpu_custom_call" | custom-call | tf_op jit(solution)/shard_map/correlate/pallas_call | solution.py:350
  (6 shorter events, 0.1 us)
Async XLA Ops:
  0.0 17.3 %copy-start.3 = (s32[32]{0:T(128)S(1)}, s32[32]{0:T(128)}, u32[]{:S(2)}) copy-start(s32[32]{0:T(128)} %param.11) | copy-start | bytes 388
  0.0 17.8 %copy-start.2 = (s32[32,16]{0,1:T(8,128)S(1)}, s32[32,16]{0,1:T(8,128)}, u32[]{:S(2)}) copy-start(s32[32,16]{0,1:T(8,128)} %param.10) | copy-start | bytes 6148
  0.0 18.0 %copy-start.4 = (s32[64]{0:T(128)S(1)}, s32[64]{0:T(128)}, u32[]{:S(2)}) copy-start(s32[64]{0:T(128)} %param.12) | copy-start | bytes 772
  8.1 19.0 %all-to-all-start = ((bf16[32,64,128]{2,1,0:T(8,128)(2,1)}), bf16[32,64,128]{2,1,0:T(8,128)(2,1)S(1)}, u32[]{:S(2)}, u32[]{:S(2)}) async-start(bf16[32,64,128]{2,1,0:T(8,128)(2,1)} %front.1), calls=%async_computation | async-start | bytes 1048576 | tf_op jit(solution)/shard_map/all_to_all | solution.py:370
  81.9 4.7 %copy-start = (bf16[2,256,1024]{2,1,0:T(8,128)(2,1)S(1)}, bf16[2,256,1024]{2,1,0:T(8,128)(2,1)}, u32[]{:S(2)}) copy-start(bf16[2,256,1024]{2,1,0:T(8,128)(2,1)} %constant.59.clone.table_ref) | copy-start | bytes 3145732
  81.9 4.7 %copy-start.1 = (bf16[16,256]{1,0:T(8,128)(2,1)S(1)}, bf16[16,256]{1,0:T(8,128)(2,1)}, u32[]{:S(2)}) copy-start(bf16[16,256]{1,0:T(8,128)(2,1)} %constant.58.clone.mask_ref) | copy-start | bytes 24580
  82.2 4.4 %collective-permute-start = (bf16[128,64,128]{2,1,0:T(8,128)(2,1)S(1)}, bf16[128,64,128]{2,1,0:T(8,128)(2,1)S(1)}, u32[]{:S(2)}, u32[]{:S(2)}) collective-permute-start(bf16[128,64,128]{2,1,0:T(8,128)(2,1)S(1)} %slice.4), channel_id=1, source_target_pairs={{0,1},{1,0},{2,3},{3,2},{4,5},{5,4},{6,7},{7,6},{8,9},{9,8},{10,11... | collective-permute-start | bytes 6291464 | tf_op jit(solution)/shard_map/ppermute | solution.py:373

commit v3 on v2

--- a/solution.py
+++ b/solution.py
@@ -34,35 +34,12 @@
 def dft_tables():
     run = SAMPLES // RADIX
     ring = 2.0 * math.pi / SAMPLES * np.arange(SAMPLES)
-    bins = bin_order().reshape(RADIX // 2, 2, FREQS // RADIX)
-    table = np.zeros((RADIX // 2, 2, run, 2, 2, FREQS // RADIX))
-    for unit in range(RADIX // 2):
-        for side in range(2):
-            phase = np.outer(np.arange(run), BAND_START + bins[unit, side]) % SAMPLES
-            cosine, sine = np.cos(ring)[phase], np.sin(ring)[phase]
-            if unit == 0:
-                table[unit, side, :, 0, side] = cosine
-                table[unit, side, :, 1, side] = -sine
-            else:
-                sign = 1.0 if side == 0 else -1.0
-                table[unit, 0, :, 0, side] = cosine
-                table[unit, 0, :, 1, side] = -sine
-                table[unit, 1, :, 0, side] = -sign * sine
-                table[unit, 1, :, 1, side] = -sign * cosine
-    table = table.reshape(RADIX // 2, 2 * run, BLOCK)
+    bins = bin_order().reshape(RADIX // 2, 1, 2 * FREQS // RADIX)
+    phase = np.arange(run)[None, :, None] * (BAND_START + bins) % SAMPLES
+    table = np.concatenate([np.cos(ring)[phase], -np.sin(ring)[phase]], axis=2)
     high = table.astype(np.float32).astype(ml_dtypes.bfloat16)
     low = (table - high.astype(np.float64)).astype(np.float32).astype(ml_dtypes.bfloat16)
     return np.concatenate([high, low], axis=2)
-
-
-def band_tables():
-    bins = bin_order()
-    near = np.abs(bins[:, None] - bins[None, :]) <= HALF
-    order = np.arange(FREQS)[:, None] == bins[None, :]
-    return (
-        near.astype(ml_dtypes.bfloat16),
-        order.astype(ml_dtypes.bfloat16),
-    )
 
 
 def lag_tables():
@@ -127,9 +104,14 @@
     ]
 
 
+def bin_of(column):
+    unit, side, group = column >> 6, (column >> 5) & 1, column & 31
+    other = jnp.where(unit == 0, RADIX // 2, RADIX - unit)
+    return RADIX * group + jnp.where(side == 0, unit, other)
+
+
 def front_kernel(
-    rows_hbm, dft_hbm, band_hbm, order_hbm, out_ref,
-    rows_ref, dft_ref, band_ref, order_ref, sums_ref, row_sem, table_sem,
+    rows_hbm, dft_hbm, out_ref, rows_ref, dft_ref, band_ref, order_ref, sums_ref, row_sem, table_sem
 ):
     each = BLOCK * BLOCK // FETCHES
     copies = []
@@ -139,13 +121,17 @@
             pltpu.make_async_copy(rows_hbm.at[part], rows_ref.at[part], row_sem.at[fetch])
         )
         copies[fetch].start()
-    fetched = [(dft_hbm, dft_ref), (band_hbm, band_ref), (order_hbm, order_ref)]
-    tables = [
-        pltpu.make_async_copy(source, target, table_sem.at[which])
-        for which, (source, target) in enumerate(fetched)
-    ]
-    for table in tables:
-        table.start()
+    table = pltpu.make_async_copy(dft_hbm, dft_ref, table_sem)
+    table.start()
+    down = lax.broadcasted_iota(jnp.int32, (FREQS, BLOCK), 0)
+    across = lax.broadcasted_iota(jnp.int32, (FREQS, BLOCK), 1)
+    bins = bin_of(down)
+    for tile in range(FREQS // BLOCK):
+        lanes = slice(tile * BLOCK, (tile + 1) * BLOCK)
+        column = bin_of(across[:8] + tile * BLOCK)[:1]
+        near = jnp.abs(bins - column) <= HALF
+        band_ref[:, lanes] = jnp.where(near, 1.0, 0.0).astype(jnp.bfloat16)
+        order_ref[:, lanes] = jnp.where(down == column, 1.0, 0.0).astype(jnp.bfloat16)
 
     def channel(chan, carry):
         x = []
@@ -163,24 +149,34 @@
         count = BLOCK // FETCHES
         lax.fori_loop(count * fetch, count * (fetch + 1), channel, 0, unroll=4)
 
-    for table in tables:
-        table.wait()
+    lane = lax.broadcasted_iota(jnp.int32, (1, BLOCK), 1)
+    sign = jnp.where((lane < 32) | (lane >= 96), 1.0, -1.0)
+    table.wait()
     found = []
     for unit in range(RADIX // 2):
-        columns = []
+        tiles = []
         for side in range(2):
-            for tile in range(4):
-                part = [
-                    sums_ref[2 * unit + side, pl.ds(2 * tile + seg, BLOCK, stride=8), :]
-                    for seg in range(2)
-                ]
-                columns.append(jnp.concatenate(part, axis=0))
-        exact = jnp.concatenate(columns, axis=1)
+            for seg in range(2):
+                tiles.append(
+                    jnp.concatenate(
+                        [
+                            sums_ref[2 * unit + side, pl.ds(2 * tile + seg, BLOCK, stride=8), :]
+                            for tile in range(4)
+                        ],
+                        axis=1,
+                    )
+                )
+        exact = jnp.concatenate(tiles, axis=0)
         high = exact.astype(jnp.bfloat16)
         low = (exact - high.astype(jnp.float32)).astype(jnp.bfloat16)
         first = jnp.dot(high, dft_ref[unit], preferred_element_type=jnp.float32)
         rest = jnp.dot(low, dft_ref[unit, :, :BLOCK], preferred_element_type=jnp.float32)
-        found.append(first[:, :BLOCK] + (first[:, BLOCK:] + rest))
+        both = first[:, :BLOCK] + (first[:, BLOCK:] + rest)
+        one, two = both[: 2 * BLOCK], both[2 * BLOCK :]
+        if unit == 0:
+            found.append(jnp.where((lane >> 5) & 1 == 0, one, two))
+        else:
+            found.append(one + sign * pltpu.roll(two, 64, 1))
     left = lax.broadcasted_iota(jnp.int32, (2 * BLOCK, BLOCK), 1) < 64
     real = []
     imag = []
@@ -224,7 +220,7 @@
             rows_ref[core, block] = twice.T.astype(jnp.bfloat16)
         return carry
 
-    lax.fori_loop(0, NBLK, turn, 0)
+    lax.fori_loop(0, NBLK, turn, 0, unroll=8)
 
     def send(chan, carry):
         slots = [SLOT_DEV * chan + slot for slot in range(SLOT_DEV)]
@@ -242,7 +238,7 @@
             out_ref[dest, pl.ds(64, 32), :] = jnp.where(left, one, two)
         return carry
 
-    lax.fori_loop(0, NBLK, send, 0)
+    lax.fori_loop(0, NBLK, send, 0, unroll=8)
 
 
 def correlate_kernel(
@@ -307,29 +303,27 @@
 
 
 def front(traces):
-    band, order = band_tables()
     rows = traces.reshape(BLOCK, 2, SAMPLES // BLOCK, BLOCK).transpose(0, 2, 1, 3)
     rows = rows.reshape(BLOCK * BLOCK, BLOCK)
-    vmem = pl.BlockSpec(memory_space=pltpu.VMEM)
     return pl.pallas_call(
         front_kernel,
         out_shape=jax.ShapeDtypeStruct((NBLK, 4 * GROUP, BLOCK), jnp.bfloat16),
-        in_specs=[pl.BlockSpec(memory_space=pltpu.HBM)] * 4,
-        out_specs=vmem,
+        in_specs=[pl.BlockSpec(memory_space=pltpu.HBM)] * 2,
+        out_specs=pl.BlockSpec(memory_space=pltpu.VMEM),
         scratch_shapes=[
             pltpu.VMEM((BLOCK * BLOCK, BLOCK), jnp.bfloat16),
-            pltpu.VMEM((RADIX // 2, 1024, 2 * BLOCK), jnp.bfloat16),
+            pltpu.VMEM((RADIX // 2, SAMPLES // RADIX, 2 * BLOCK), jnp.bfloat16),
             pltpu.VMEM((FREQS, FREQS), jnp.bfloat16),
             pltpu.VMEM((FREQS, FREQS), jnp.bfloat16),
             pltpu.VMEM((RADIX, 8 * BLOCK, BLOCK), jnp.float32),
             pltpu.SemaphoreType.DMA((FETCHES,)),
-            pltpu.SemaphoreType.DMA((3,)),
+            pltpu.SemaphoreType.DMA,
         ],
         compiler_params=pltpu.CompilerParams(vmem_limit_bytes=VMEM),
         name="front",
     )(
-        *[pltpu.with_memory_space_constraint(jnp.asarray(each), pltpu.HBM)
-          for each in (rows, dft_tables(), band, order)]
+        pltpu.with_memory_space_constraint(rows, pltpu.HBM),
+        pltpu.with_memory_space_constraint(jnp.asarray(dft_tables()), pltpu.HBM),
     )
 
 

time: 97.6 us -> 94.2 us (0.965)
  Pallas kernels: 23.3 us -> 19.8 us
    pallas_call x1, Pallas kernels: 4.65 us -> 1.99 us  [select(): pl.pallas_call(select_kernel, out_shape=jax.ShapeDtypeStruct((128, 96, BL...]
where the time goes in v3:
time: 94.2 us; the launch traced here: 93.9 us
  blocking collectives  50.1 us (53%)
  Pallas kernels  19.8 us (21%)
  waiting for transfers between devices  13.1 us (14%)
  starting transfers between devices  9.5 us (10%)
    all_to_all x1, blocking collectives, on_device(): lax.all_to_all(sent, ('chan', 'seg'), split_axis=0, concat_axis=0, tiled=...  50.1 us
    pallas_call x1, Pallas kernels, correlate(): pl.pallas_call(correlate_kernel, out_shape=jax.ShapeDtypeStruct((32, SLOT...  10.6 us
    all_to_all x1, starting transfers between devices, on_device(): lax.all_to_all(front(traces), 'chan', split_axis=0, concat_axis=0, tiled=...  9.24 us
    all_to_all x1, waiting for transfers between devices, on_device(): lax.all_to_all(front(traces), 'chan', split_axis=0, concat_axis=0, tiled=...  8.93 us
    pallas_call x1, Pallas kernels, front(): pl.pallas_call(front_kernel, out_shape=jax.ShapeDtypeStruct((NBLK, 4 * GR...  7.26 us
    ppermute x1, waiting for transfers between devices, on_device(): other = lax.ppermute(own[:, :64], 'seg', [(0, 1), (1, 0), (2, 3), (3, 2)])  4.14 us
    pallas_call x1, Pallas kernels, select(): pl.pallas_call(select_kernel, out_shape=jax.ShapeDtypeStruct((128, 96, BL...  1.99 us
  transfers between devices with their start and end apart: 2, of which 2 were waited for; matrix products, arithmetic and copies ran while one was open for 1% of the time, Pallas kernels for 0%

profile of v3, /device:TPU:1, one launch (start us, length us, event | category | flops | bytes accessed | tf_op | source)
XLA Modules:
  0.0 93.9 jit_solution(18316545282770999165)
XLA Ops:
  0.0 0.0 copy-start.3
  0.0 0.0 copy-start.2
  0.0 0.0 copy-start.4
  0.0 7.3 %front.1 = bf16[32,64,128]{2,1,0:T(8,128)(2,1)} custom-call(bf16[16384,128]{1,0:T(8,128)(2,1)} %bitcast.7, bf16[8,512,256]{2,1,0:T(8,128)(2,1)} %constant.51.clone.dft_hbm), custom_call_target="tpu_custom_call" | custom-call | tf_op jit(solution)/shard_map/front/pallas_call | solution.py:308
  7.3 9.2 %all-to-all-start = ((bf16[32,64,128]{2,1,0:T(8,128)(2,1)}), bf16[32,64,128]{2,1,0:T(8,128)(2,1)S(1)}, u32[]{:S(2)}, u32[]{:S(2)}) async-start(bf16[32,64,128]{2,1,0:T(8,128)(2,1)} %front.1), calls=%async_computation | async-start | bytes 1048576 | tf_op jit(solution)/shard_map/all_to_all | solution.py:364
  16.5 0.0 copy-done.3
  16.5 0.1 copy.14
  16.6 0.1 reduce-window.9
  16.7 0.1 reduce
  16.8 0.1 convert_reduce_fusion
  16.9 0.1 select_reduce_fusion.3
  17.0 0.0 copy-done.2
  17.0 0.1 copy.15
  17.1 0.1 select_reduce_fusion
  17.3 0.0 copy-done.4
  17.3 0.1 select_reduce_fusion.1
  17.4 8.9 %all-to-all-done.held_ref = bf16[32,64,128]{2,1,0:T(8,128)(2,1)S(1)} async-done(((bf16[32,64,128]{2,1,0:T(8,128)(2,1)}), bf16[32,64,128]{2,1,0:T(8,128)(2,1)S(1)}, u32[]{:S(2)}, u32[]{:S(2)}) %all-to-all-start) | async-done | bytes 524320 | tf_op jit(solution)/shard_map/all_to_all | solution.py:364
  26.3 2.0 %select.11 = bf16[128,96,128]{2,1,0:T(8,128)(2,1)S(1)} custom-call(s32[64]{0:T(128)S(1)} %get-tuple-element.6.first_ref, s32[64]{0:T(128)S(1)} %get-tuple-element.5.second_ref, s32[1]{0:T(128)} %bitcast.place_ref, bf16[32,64,128]{2,1,0:T(8,128)(2,1)S(1)} %all-to-all-done.held_ref), custom_call_target="tpu_custom_call" | custom-call | tf_op jit(solution)/shard_map/select/pallas_call | solution.py:332
  28.3 50.1 %all_to_all.10.own_ref = bf16[128,96,128]{2,1,0:T(8,128)(2,1)S(1)} all-to-all(bf16[128,96,128]{2,1,0:T(8,128)(2,1)S(1)} %select.11), channel_id=1, replica_groups=mesh['chan'=32,'seg'=4] {'chan','seg'}, dimensions={0} | all-to-all | bytes 6291456 | tf_op jit(solution)/shard_map/all_to_all | solution.py:366
  78.4 0.0 copy-start
  78.4 0.0 copy-start.1
  78.4 0.3 slice.4
  78.8 0.3 collective-permute-start
  79.0 4.1 %collective-permute-done.other_ref = bf16[128,64,128]{2,1,0:T(8,128)(2,1)S(1)} collective-permute-done((bf16[128,64,128]{2,1,0:T(8,128)(2,1)S(1)}, bf16[128,64,128]{2,1,0:T(8,128)(2,1)S(1)}, u32[]{:S(2)}, u32[]{:S(2)}) %collective-permute-start) | collective-permute-done | bytes 2097184 | tf_op jit(solution)/shard_map/ppermute | solution.py:367
  83.2 0.0 copy-done
  83.2 0.0 copy-done.1
  83.2 10.6 %correlate.1 = f32[32,2,128,256]{3,2,1,0:T(8,128)} custom-call(s32[1]{0:T(128)S(6)} %select_n.36.core_ref, bf16[128,96,128]{2,1,0:T(8,128)(2,1)S(1)} %all_to_all.10.own_ref, bf16[128,64,128]{2,1,0:T(8,128)(2,1)S(1)} %collective-permute-done.other_ref, bf16[16,256]{1,0:T(8,128)(2,1)S(1)} %copy-done.1, bf16[2,256,1024]{2,1,0:T(8,128)(2,1)S(1)} %copy-done), custom_call_target="tpu_custom_call" | custom-call | tf_op jit(solution)/shard_map/correlate/pallas_call | solution.py:344
  (6 shorter events, 0.1 us)
Async XLA Ops:
  0.0 16.5 %copy-start.3 = (s32[32]{0:T(128)S(1)}, s32[32]{0:T(128)}, u32[]{:S(2)}) copy-start(s32[32]{0:T(128)} %param.9) | copy-start | bytes 388
  0.0 17.0 %copy-start.2 = (s32[32,16]{0,1:T(8,128)S(1)}, s32[32,16]{0,1:T(8,128)}, u32[]{:S(2)}) copy-start(s32[32,16]{0,1:T(8,128)} %param.8) | copy-start | bytes 6148
  0.0 17.3 %copy-start.4 = (s32[64]{0:T(128)S(1)}, s32[64]{0:T(128)}, u32[]{:S(2)}) copy-start(s32[64]{0:T(128)} %param.10) | copy-start | bytes 772
  7.3 19.0 %all-to-all-start = ((bf16[32,64,128]{2,1,0:T(8,128)(2,1)}), bf16[32,64,128]{2,1,0:T(8,128)(2,1)S(1)}, u32[]{:S(2)}, u32[]{:S(2)}) async-start(bf16[32,64,128]{2,1,0:T(8,128)(2,1)} %front.1), calls=%async_computation | async-start | bytes 1048576 | tf_op jit(solution)/shard_map/all_to_all | solution.py:364
  78.4 4.7 %copy-start = (bf16[2,256,1024]{2,1,0:T(8,128)(2,1)S(1)}, bf16[2,256,1024]{2,1,0:T(8,128)(2,1)}, u32[]{:S(2)}) copy-start(bf16[2,256,1024]{2,1,0:T(8,128)(2,1)} %constant.53.clone.table_ref) | copy-start | bytes 3145732
  78.4 4.7 %copy-start.1 = (bf16[16,256]{1,0:T(8,128)(2,1)S(1)}, bf16[16,256]{1,0:T(8,128)(2,1)}, u32[]{:S(2)}) copy-start(bf16[16,256]{1,0:T(8,128)(2,1)} %constant.52.clone.mask_ref) | copy-start | bytes 24580
  78.8 4.4 %collective-permute-start = (bf16[128,64,128]{2,1,0:T(8,128)(2,1)S(1)}, bf16[128,64,128]{2,1,0:T(8,128)(2,1)S(1)}, u32[]{:S(2)}, u32[]{:S(2)}) collective-permute-start(bf16[128,64,128]{2,1,0:T(8,128)(2,1)S(1)} %slice.4), channel_id=1, source_target_pairs={{0,1},{1,0},{2,3},{3,2},{4,5},{5,4},{6,7},{7,6},{8,9},{9,8},{10,11... | collective-permute-start | bytes 6291464 | tf_op jit(solution)/shard_map/ppermute | solution.py:367

commit v4 on v3

--- a/solution.py
+++ b/solution.py
@@ -22,7 +22,7 @@
 RADIX = 16
 VMEM = 32 * 1024 * 1024
 PAIRS = 4
-UNROLL = 32
+UNROLL = 16
 FETCHES = 8
 
 
@@ -49,15 +49,15 @@
     norm = 1.0 / math.sqrt(FREQS * SEGS)
     parts = np.stack([np.cos(angles), -np.sin(angles)]).astype(ml_dtypes.bfloat16)
     parts = (parts.astype(np.float32) * norm).astype(ml_dtypes.bfloat16)
-    parts = parts.reshape(2, FREQS // GROUP, 2, GROUP // 2, LAGS).transpose(4, 1, 0, 2, 3)
-    both = np.stack([parts, parts[:, :, :, ::-1]])
+    parts = parts.reshape(2, NBLK // 2, 2, 2, GROUP // 2, LAGS).transpose(5, 3, 1, 0, 2, 4)
+    both = np.stack([parts, parts[:, ::-1]])
     return both.reshape(2, LAGS, 2 * FREQS)
 
 
 def group_mask():
-    lane = np.arange(256)
-    own = (lane // 16 % 2) * 8 + lane % 8
-    return (np.arange(GROUP)[:, None] == own[None, :]).astype(ml_dtypes.bfloat16)
+    lane, row = np.arange(256)[None, :], np.arange(GROUP)[:, None]
+    same = (lane // 128 == row // 8) & (lane % 8 == row % 8)
+    return same.astype(ml_dtypes.bfloat16)
 
 
 def pair_blocks(pair_offsets, pair_counts, pair_owner, block_count, slot_count):
@@ -208,16 +208,15 @@
 
 def select_kernel(first_ref, second_ref, place_ref, held_ref, out_ref, rows_ref):
     lane = lax.broadcasted_iota(jnp.int32, (32, BLOCK), 1)
-    left = (lane < 64) == (place_ref[0] % 2 == 0)
+    place = place_ref[0]
+    left = (((lane >> 5) - place) & 3) < 2
 
     def turn(block, carry):
         tiles = held_ref[block].astype(jnp.float32)
-        for core in range(2):
-            order = tiles if core == 0 else jnp.concatenate(
-                [tiles[16:32], tiles[0:16], tiles[48:64], tiles[32:48]], axis=0
-            )
-            twice = jnp.concatenate([order, order], axis=0)
-            rows_ref[core, block] = twice.T.astype(jnp.bfloat16)
+        halves = [[tiles[0:16], tiles[32:48]], [tiles[16:32], tiles[48:64]]]
+        for lead in range(2):
+            order = halves[lead] + halves[1 - lead]
+            rows_ref[lead, block] = jnp.concatenate(order + order, axis=0).T.astype(jnp.bfloat16)
         return carry
 
     lax.fori_loop(0, NBLK, turn, 0, unroll=8)
@@ -233,63 +232,85 @@
                     out_ref[dest, pl.ds(32 * slot + 16 * part, 16), :] = held_ref[
                         second, pl.ds(32 * part + 16 * core, 16), :
                     ]
-            one = rows_ref[core, first_ref[slots[0]], pl.ds(32 * seg, 32), :]
-            two = rows_ref[core, first_ref[slots[1]], pl.ds(32 * seg, 32), :]
+            lead = (place & 1) ^ core
+            one = rows_ref[lead, first_ref[slots[0]], pl.ds(32 * seg, 32), :]
+            two = rows_ref[lead, first_ref[slots[1]], pl.ds(32 * seg, 32), :]
             out_ref[dest, pl.ds(64, 32), :] = jnp.where(left, one, two)
         return carry
 
     lax.fori_loop(0, NBLK, send, 0, unroll=8)
 
 
+def cross_of(slot, half, pair, second_ref, own_ref, mask):
+    lane = lax.broadcasted_iota(jnp.int32, (32, BLOCK), 1) >> 5
+    place = 2 * slot + half
+    upper = []
+    lower = []
+    first = []
+    for group in range(2):
+        lanes = None
+        for block in range(4):
+            src = 8 * pair + 4 * group + (block - place) % 4
+            real = second_ref[src, pl.ds(32 * slot, 16), :]
+            imag = second_ref[src, pl.ds(32 * slot + 16, 16), :]
+            upper += [real, imag]
+            lower += [-imag, real]
+            piece = own_ref[src, pl.ds(64, 32), :]
+            lanes = piece if lanes is None else jnp.where(lane == block, piece, lanes)
+        first.append(lanes)
+    second = jnp.concatenate(
+        [jnp.concatenate(upper, axis=0), jnp.concatenate(lower, axis=0)], axis=1
+    )
+    first = jnp.concatenate(first, axis=1)
+    spread = [jnp.broadcast_to(first[i : i + 1], (GROUP, 256)) * mask for i in range(32)]
+    found = jnp.dot(
+        jnp.concatenate(spread, axis=0), second, preferred_element_type=jnp.float32
+    ).astype(jnp.bfloat16)
+    return [
+        found[:, part * BLOCK : (part + 1) * BLOCK].reshape(32, GROUP, BLOCK) for part in range(2)
+    ]
+
+
+def near_kernel(own_ref, mask_ref, cross_ref):
+    for slot in range(SLOT_DEV):
+
+        def cross(pair, carry):
+            for part, found in enumerate(cross_of(slot, 0, pair, own_ref, own_ref, mask_ref[...])):
+                cross_ref[slot, :, 2 * pair + part] = found
+            return carry
+
+        lax.fori_loop(0, NBLK // 2, cross, 0, unroll=UNROLL)
+
+
 def correlate_kernel(
-    core_ref, own_ref, other_ref, mask_ref, table_ref, out_hbm, cross_ref, lag_ref, out_sem
+    core_ref, own_ref, other_ref, near_ref, mask_ref, table_ref, out_hbm, cross_ref, lag_ref, out_sem
 ):
     core = core_ref[0]
     leaving = []
     for slot in range(SLOT_DEV):
 
-        def cross(group, carry):
-            order = [slot, 1 - slot, 2 + slot, 3 - slot]
-            upper = []
-            lower = []
-            for seg in order:
-                src = 4 * group + seg
-                tiles = []
-                for part in range(2):
-                    rows = pl.ds(32 * slot + 16 * part, 16)
-                    tiles.append([own_ref[src, rows, :], other_ref[src, rows, :]])
-                upper += tiles[0] + tiles[1]
-                lower += [-tiles[1][0], -tiles[1][1]] + tiles[0]
-            second = jnp.concatenate(
-                [jnp.concatenate(upper, axis=0), jnp.concatenate(lower, axis=0)], axis=1
-            )
-            lane = lax.broadcasted_iota(jnp.int32, (32, BLOCK), 1)
-            left = (lane < 64) == (slot == 0)
-            lanes = [own_ref[4 * group + seg, pl.ds(64, 32), :] for seg in range(4)]
-            first = jnp.concatenate(
-                [jnp.where(left, lanes[0], lanes[1]), jnp.where(left, lanes[2], lanes[3])], axis=1
-            )
-            mask = mask_ref[...]
-            spread = [jnp.broadcast_to(first[i : i + 1], (GROUP, 256)) * mask for i in range(32)]
-            found = jnp.dot(
-                jnp.concatenate(spread, axis=0), second, preferred_element_type=jnp.float32
-            ).astype(jnp.bfloat16)
-            for part in range(2):
-                cross_ref[:, 2 * group + part] = found[
-                    :, part * BLOCK : (part + 1) * BLOCK
-                ].reshape(32, GROUP, BLOCK)
+        def cross(pair, carry):
+            for part, found in enumerate(
+                cross_of(slot, 1, pair, other_ref, own_ref, mask_ref[...])
+            ):
+                cross_ref[:, 2 * pair + part] = found
             return carry
 
         def lags(pair, carry):
-            sides = [cross_ref[2 * pair + k].reshape(2 * FREQS, BLOCK) for k in range(2)]
+            sides = []
+            for k in range(2):
+                near = near_ref[slot, 2 * pair + k].reshape(FREQS, BLOCK)
+                far = cross_ref[2 * pair + k].reshape(FREQS, BLOCK)
+                sides.append(jnp.concatenate([near, far], axis=0))
             lagged = jnp.dot(
                 table_ref[core], jnp.concatenate(sides, axis=1), preferred_element_type=jnp.float32
             )
+            both = lagged.T
             for k in range(2):
-                lag_ref[slot, 2 * pair + k] = lagged[:, k * BLOCK : (k + 1) * BLOCK].T
+                lag_ref[slot, 2 * pair + k] = both[k * BLOCK : (k + 1) * BLOCK]
             return carry
 
-        lax.fori_loop(0, NBLK, cross, 0, unroll=UNROLL)
+        lax.fori_loop(0, NBLK // 2, cross, 0, unroll=UNROLL)
         for step in range(16 // PAIRS):
             lax.fori_loop(PAIRS * step, PAIRS * (step + 1), lags, 0, unroll=True)
             rows = pl.ds(2 * PAIRS * step, 2 * PAIRS)
@@ -339,21 +360,35 @@
     )(slot_first, slot_second, place, held)
 
 
-def correlate(core, own, other):
+def near_cross(own):
+    vmem = pl.BlockSpec(memory_space=pltpu.VMEM)
+    return pl.pallas_call(
+        near_kernel,
+        out_shape=jax.ShapeDtypeStruct((SLOT_DEV, 32, NBLK, GROUP, BLOCK), jnp.bfloat16),
+        in_specs=[vmem, vmem],
+        out_specs=vmem,
+        compiler_params=pltpu.CompilerParams(vmem_limit_bytes=16 * 1024 * 1024),
+        cost_estimate=pl.CostEstimate(flops=8 << 30, transcendentals=0, bytes_accessed=11 << 20),
+        name="near_cross",
+    )(own, jnp.asarray(group_mask()))
+
+
+def correlate(core, own, other, near=None):
+    near = near_cross(own) if near is None else near
     vmem = pl.BlockSpec(memory_space=pltpu.VMEM)
     return pl.pallas_call(
         correlate_kernel,
         out_shape=jax.ShapeDtypeStruct((32, SLOT_DEV, BLOCK, LAGS), jnp.float32),
-        in_specs=[pl.BlockSpec(memory_space=pltpu.SMEM), vmem, vmem, vmem, vmem],
+        in_specs=[pl.BlockSpec(memory_space=pltpu.SMEM)] + [vmem] * 5,
         out_specs=pl.BlockSpec(memory_space=pl.ANY),
         scratch_shapes=[
-            pltpu.VMEM((32, 2 * FREQS // GROUP, GROUP, BLOCK), jnp.bfloat16),
+            pltpu.VMEM((32, NBLK, GROUP, BLOCK), jnp.bfloat16),
             pltpu.VMEM((SLOT_DEV, 32, BLOCK, LAGS), jnp.float32),
             pltpu.SemaphoreType.DMA((SLOT_DEV, 16 // PAIRS)),
         ],
-        compiler_params=pltpu.CompilerParams(vmem_limit_bytes=VMEM),
+        compiler_params=pltpu.CompilerParams(vmem_limit_bytes=24 * 1024 * 1024),
         name="correlate",
-    )(core, own, other, jnp.asarray(group_mask()), jnp.asarray(lag_tables()))
+    )(core, own, other, near, jnp.asarray(group_mask()), jnp.asarray(lag_tables()))
 
 
 def on_device(traces, pair_offsets, pair_counts, pair_owner):
@@ -365,7 +400,7 @@
     sent = select(slot_first, slot_second, seg, held)
     own = lax.all_to_all(sent, ("chan", "seg"), split_axis=0, concat_axis=0, tiled=True)
     other = lax.ppermute(own[:, :64], "seg", [(0, 1), (1, 0), (2, 3), (3, 2)])
-    return correlate(seg % 2, own, other)
+    return correlate(seg % 2, own, other, near_cross(own))
 
 
 def solution(mesh):

time: 94.2 us -> 91.9 us (0.976)
  waiting for transfers between devices: 13.1 us -> 10.5 us
    ppermute x1, waiting for transfers between devices: 4.14 us -> 1.62 us  [on_device(): other = lax.ppermute(own[:, :64], 'seg', [(0, 1), (1, 0), (2, 3), (3, 2)])]
    pallas_call x0 -> x1, Pallas kernels: none -> 2.35 us  [near_cross(): pl.pallas_call(near_kernel, out_shape=jax.ShapeDtypeStruct((SLOT_DEV, 32,...]
    pallas_call x1, Pallas kernels: 10.6 us -> 8.23 us  [correlate(): pl.pallas_call(correlate_kernel, out_shape=jax.ShapeDtypeStruct((32, SLOT...]
  transfers between devices with their start and end apart: 2 -> 2, of which waited for: 2 -> 2; matrix products, arithmetic and copies ran while one was open for 1% -> 1% of each run, Pallas kernels for 0% -> 3%
where the time goes in v4:
time: 91.9 us; the launch traced here: 91.6 us
  blocking collectives  50.1 us (55%)
  Pallas kernels  20 us (22%)
  waiting for transfers between devices  10.5 us (11%)
  starting transfers between devices  9.5 us (10%)
    all_to_all x1, blocking collectives, on_device(): lax.all_to_all(sent, ('chan', 'seg'), split_axis=0, concat_axis=0, tiled=...  50.1 us
    all_to_all x1, starting transfers between devices, on_device(): lax.all_to_all(front(traces), 'chan', split_axis=0, concat_axis=0, tiled=...  9.24 us
    all_to_all x1, waiting for transfers between devices, on_device(): lax.all_to_all(front(traces), 'chan', split_axis=0, concat_axis=0, tiled=...  8.93 us
    pallas_call x1, Pallas kernels, correlate(): pl.pallas_call(correlate_kernel, out_shape=jax.ShapeDtypeStruct((32, SLOT...  8.23 us
    pallas_call x1, Pallas kernels, front(): pl.pallas_call(front_kernel, out_shape=jax.ShapeDtypeStruct((NBLK, 4 * GR...  7.26 us
    pallas_call x1, Pallas kernels, near_cross(): pl.pallas_call(near_kernel, out_shape=jax.ShapeDtypeStruct((SLOT_DEV, 32,...  2.35 us
    pallas_call x1, Pallas kernels, select(): pl.pallas_call(select_kernel, out_shape=jax.ShapeDtypeStruct((128, 96, BL...  2.12 us
  transfers between devices with their start and end apart: 2, of which 2 were waited for; matrix products, arithmetic and copies ran while one was open for 1% of the time, Pallas kernels for 3%

profile of v4, /device:TPU:1, one launch (start us, length us, event | category | flops | bytes accessed | tf_op | source)
XLA Modules:
  0.0 91.6 jit_solution(428780737615895771)
XLA Ops:
  0.0 0.0 copy-start.3
  0.0 0.0 copy-start.2
  0.0 0.0 copy-start.4
  0.0 7.3 %front.1 = bf16[32,64,128]{2,1,0:T(8,128)(2,1)} custom-call(bf16[16384,128]{1,0:T(8,128)(2,1)} %bitcast.7, bf16[8,512,256]{2,1,0:T(8,128)(2,1)} %constant.51.clone.dft_hbm), custom_call_target="tpu_custom_call" | custom-call | tf_op jit(solution)/shard_map/front/pallas_call | solution.py:329
  7.3 9.2 %all-to-all-start = ((bf16[32,64,128]{2,1,0:T(8,128)(2,1)}), bf16[32,64,128]{2,1,0:T(8,128)(2,1)S(1)}, u32[]{:S(2)}, u32[]{:S(2)}) async-start(bf16[32,64,128]{2,1,0:T(8,128)(2,1)} %front.1), calls=%async_computation | async-start | bytes 1048576 | tf_op jit(solution)/shard_map/all_to_all | solution.py:399
  16.5 0.0 copy-done.3
  16.5 0.1 copy.15
  16.6 0.1 reduce-window.9
  16.7 0.1 reduce
  16.8 0.1 convert_reduce_fusion
  16.9 0.1 select_reduce_fusion.3
  17.0 0.0 copy-done.2
  17.0 0.1 copy.16
  17.1 0.1 select_reduce_fusion
  17.3 0.0 copy-done.4
  17.3 0.1 select_reduce_fusion.1
  17.4 8.9 %all-to-all-done.held_ref = bf16[32,64,128]{2,1,0:T(8,128)(2,1)S(1)} async-done(((bf16[32,64,128]{2,1,0:T(8,128)(2,1)}), bf16[32,64,128]{2,1,0:T(8,128)(2,1)S(1)}, u32[]{:S(2)}, u32[]{:S(2)}) %all-to-all-start) | async-done | bytes 524320 | tf_op jit(solution)/shard_map/all_to_all | solution.py:399
  26.3 2.1 %select.11 = bf16[128,96,128]{2,1,0:T(8,128)(2,1)S(1)} custom-call(s32[64]{0:T(128)S(1)} %get-tuple-element.6.first_ref, s32[64]{0:T(128)S(1)} %get-tuple-element.5.second_ref, s32[1]{0:T(128)} %bitcast.place_ref, bf16[32,64,128]{2,1,0:T(8,128)(2,1)S(1)} %all-to-all-done.held_ref), custom_call_target="tpu_custom_call" | custom-call | tf_op jit(solution)/shard_map/select/pallas_call | solution.py:353
  28.4 50.1 %all_to_all.10.own_ref = bf16[128,96,128]{2,1,0:T(8,128)(2,1)S(1)} all-to-all(bf16[128,96,128]{2,1,0:T(8,128)(2,1)S(1)} %select.11), channel_id=1, replica_groups=mesh['chan'=32,'seg'=4] {'chan','seg'}, dimensions={0} | all-to-all | bytes 6291456 | tf_op jit(solution)/shard_map/all_to_all | solution.py:401
  78.6 0.0 copy-start.1
  78.6 0.2 slice.4
  78.8 0.3 collective-permute-start
  79.1 0.2 copy-done.1
  79.3 0.0 copy-start
  79.3 2.4 %near_cross.1.near_ref = bf16[2,32,32,16,128]{4,3,2,1,0:T(8,128)(2,1)S(1)} custom-call(bf16[128,96,128]{2,1,0:T(8,128)(2,1)S(1)} %all_to_all.10.own_ref, bf16[16,256]{1,0:T(8,128)(2,1)S(1)} %copy-done.1), custom_call_target="tpu_custom_call" | custom-call | flops 8589934592 | bytes 11534336 | tf_op jit(solution)/shard_map/near_cross/pallas_call | solution.py:365
  81.6 1.6 %collective-permute-done.other_ref = bf16[128,64,128]{2,1,0:T(8,128)(2,1)S(1)} collective-permute-done((bf16[128,64,128]{2,1,0:T(8,128)(2,1)S(1)}, bf16[128,64,128]{2,1,0:T(8,128)(2,1)S(1)}, u32[]{:S(2)}, u32[]{:S(2)}) %collective-permute-start) | collective-permute-done | bytes 2097184 | tf_op jit(solution)/shard_map/ppermute | solution.py:402
  83.2 0.0 copy-done
  83.2 8.2 %correlate.1 = f32[32,2,128,256]{3,2,1,0:T(8,128)} custom-call(s32[1]{0:T(128)S(6)} %select_n.36.core_ref, bf16[128,96,128]{2,1,0:T(8,128)(2,1)S(1)} %all_to_all.10.own_ref, bf16[128,64,128]{2,1,0:T(8,128)(2,1)S(1)} %collective-permute-done.other_ref, bf16[2,32,32,16,128]{4,3,2,1,0:T(8,128)(2,1)S(1)} %near_cross.1.near_ref, bf16[16,256]{1,0:T(8,128)(2,1)S(1)} %copy-done.1, ...), custom_call_target="tpu_custom_call" | custom-call | tf_op jit(solution)/shard_map/correlate/pallas_call | solution.py:379
  (6 shorter events, 0.1 us)
Async XLA Ops:
  0.0 16.5 %copy-start.3 = (s32[32]{0:T(128)S(1)}, s32[32]{0:T(128)}, u32[]{:S(2)}) copy-start(s32[32]{0:T(128)} %param.10) | copy-start | bytes 388
  0.0 17.0 %copy-start.2 = (s32[32,16]{0,1:T(8,128)S(1)}, s32[32,16]{0,1:T(8,128)}, u32[]{:S(2)}) copy-start(s32[32,16]{0,1:T(8,128)} %param.9) | copy-start | bytes 6148
  0.0 17.3 %copy-start.4 = (s32[64]{0:T(128)S(1)}, s32[64]{0:T(128)}, u32[]{:S(2)}) copy-start(s32[64]{0:T(128)} %param.11) | copy-start | bytes 772
  7.3 19.0 %all-to-all-start = ((bf16[32,64,128]{2,1,0:T(8,128)(2,1)}), bf16[32,64,128]{2,1,0:T(8,128)(2,1)S(1)}, u32[]{:S(2)}, u32[]{:S(2)}) async-start(bf16[32,64,128]{2,1,0:T(8,128)(2,1)} %front.1), calls=%async_computation | async-start | bytes 1048576 | tf_op jit(solution)/shard_map/all_to_all | solution.py:399
  78.6 0.7 copy-start.1
  78.8 4.4 %collective-permute-start = (bf16[128,64,128]{2,1,0:T(8,128)(2,1)S(1)}, bf16[128,64,128]{2,1,0:T(8,128)(2,1)S(1)}, u32[]{:S(2)}, u32[]{:S(2)}) collective-permute-start(bf16[128,64,128]{2,1,0:T(8,128)(2,1)S(1)} %slice.4), channel_id=1, source_target_pairs={{0,1},{1,0},{2,3},{3,2},{4,5},{5,4},{6,7},{7,6},{8,9},{9,8},{10,11... | collective-permute-start | bytes 6291464 | tf_op jit(solution)/shard_map/ppermute | solution.py:402
  79.3 4.0 %copy-start = (bf16[2,256,1024]{2,1,0:T(8,128)(2,1)S(1)}, bf16[2,256,1024]{2,1,0:T(8,128)(2,1)}, u32[]{:S(2)}) copy-start(bf16[2,256,1024]{2,1,0:T(8,128)(2,1)} %constant.53.clone.table_ref) | copy-start | bytes 3145732

commit v5 on v4

--- a/solution.py
+++ b/solution.py
@@ -225,7 +225,7 @@
         slots = [SLOT_DEV * chan + slot for slot in range(SLOT_DEV)]
         for seg in range(4):
             core = seg % 2
-            dest = 4 * chan + seg
+            dest = NBLK * seg + chan
             for slot in range(SLOT_DEV):
                 second = second_ref[slots[slot]]
                 for part in range(2):
@@ -250,7 +250,7 @@
     for group in range(2):
         lanes = None
         for block in range(4):
-            src = 8 * pair + 4 * group + (block - place) % 4
+            src = NBLK * ((block - place) % 4) + 2 * pair + group
             real = second_ref[src, pl.ds(32 * slot, 16), :]
             imag = second_ref[src, pl.ds(32 * slot + 16, 16), :]
             upper += [real, imag]
@@ -398,7 +398,7 @@
     seg = lax.axis_index("seg").astype(jnp.int32).reshape(1)
     held = lax.all_to_all(front(traces), "chan", split_axis=0, concat_axis=0, tiled=True)
     sent = select(slot_first, slot_second, seg, held)
-    own = lax.all_to_all(sent, ("chan", "seg"), split_axis=0, concat_axis=0, tiled=True)
+    own = lax.all_to_all(sent, ("seg", "chan"), split_axis=0, concat_axis=0, tiled=True)
     other = lax.ppermute(own[:, :64], "seg", [(0, 1), (1, 0), (2, 3), (3, 2)])
     return correlate(seg % 2, own, other, near_cross(own))
 

time: 91.9 us -> 91.9 us (level)
  starting transfers between devices: 9.5 us -> 10.5 us
    ppermute x1, starting transfers between devices: 0.27 us -> 1.3 us  [on_device(): other = lax.ppermute(own[:, :64], 'seg', [(0, 1), (1, 0), (2, 3), (3, 2)])]
where the time goes in v5:
time: 91.9 us; the launch traced here: 91.6 us
  blocking collectives  49.4 us (54%)
  Pallas kernels  20 us (22%)
  starting transfers between devices  10.5 us (11%)
  waiting for transfers between devices  10.3 us (11%)
    all_to_all x1, blocking collectives, on_device(): lax.all_to_all(sent, ('seg', 'chan'), split_axis=0, concat_axis=0, tiled=...  49.4 us
    all_to_all x1, starting transfers between devices, on_device(): lax.all_to_all(front(traces), 'chan', split_axis=0, concat_axis=0, tiled=...  9.24 us
    all_to_all x1, waiting for transfers between devices, on_device(): lax.all_to_all(front(traces), 'chan', split_axis=0, concat_axis=0, tiled=...  8.93 us
    pallas_call x1, Pallas kernels, correlate(): pl.pallas_call(correlate_kernel, out_shape=jax.ShapeDtypeStruct((32, SLOT...  8.25 us
    pallas_call x1, Pallas kernels, front(): pl.pallas_call(front_kernel, out_shape=jax.ShapeDtypeStruct((NBLK, 4 * GR...  7.26 us
    pallas_call x1, Pallas kernels, near_cross(): pl.pallas_call(near_kernel, out_shape=jax.ShapeDtypeStruct((SLOT_DEV, 32,...  2.35 us
    pallas_call x1, Pallas kernels, select(): pl.pallas_call(select_kernel, out_shape=jax.ShapeDtypeStruct((128, 96, BL...  2.12 us
  transfers between devices with their start and end apart: 2, of which 2 were waited for; matrix products, arithmetic and copies ran while one was open for 1% of the time, Pallas kernels for 3%

profile of v5, /device:TPU:1, one launch (start us, length us, event | category | flops | bytes accessed | tf_op | source)
XLA Modules:
  0.0 91.6 jit_solution(6809940707799122736)
XLA Ops:
  0.0 0.0 copy-start.3
  0.0 0.0 copy-start.2
  0.0 0.0 copy-start.4
  0.0 7.3 %front.1 = bf16[32,64,128]{2,1,0:T(8,128)(2,1)} custom-call(bf16[16384,128]{1,0:T(8,128)(2,1)} %bitcast.7, bf16[8,512,256]{2,1,0:T(8,128)(2,1)} %constant.51.clone.dft_hbm), custom_call_target="tpu_custom_call" | custom-call | tf_op jit(solution)/shard_map/front/pallas_call | solution.py:329
  7.3 9.2 %all-to-all-start = ((bf16[32,64,128]{2,1,0:T(8,128)(2,1)}), bf16[32,64,128]{2,1,0:T(8,128)(2,1)S(1)}, u32[]{:S(2)}, u32[]{:S(2)}) async-start(bf16[32,64,128]{2,1,0:T(8,128)(2,1)} %front.1), calls=%async_computation | async-start | bytes 1048576 | tf_op jit(solution)/shard_map/all_to_all | solution.py:399
  16.5 0.0 copy-done.3
  16.5 0.1 copy.15
  16.6 0.1 reduce-window.9
  16.7 0.1 reduce
  16.8 0.1 convert_reduce_fusion
  16.9 0.1 select_reduce_fusion.3
  17.0 0.0 copy-done.2
  17.0 0.1 copy.16
  17.1 0.1 select_reduce_fusion
  17.3 0.0 copy-done.4
  17.3 0.1 select_reduce_fusion.1
  17.4 8.9 %all-to-all-done.held_ref = bf16[32,64,128]{2,1,0:T(8,128)(2,1)S(1)} async-done(((bf16[32,64,128]{2,1,0:T(8,128)(2,1)}), bf16[32,64,128]{2,1,0:T(8,128)(2,1)S(1)}, u32[]{:S(2)}, u32[]{:S(2)}) %all-to-all-start) | async-done | bytes 524320 | tf_op jit(solution)/shard_map/all_to_all | solution.py:399
  26.3 2.1 %select.11 = bf16[128,96,128]{2,1,0:T(8,128)(2,1)S(1)} custom-call(s32[64]{0:T(128)S(1)} %get-tuple-element.6.first_ref, s32[64]{0:T(128)S(1)} %get-tuple-element.5.second_ref, s32[1]{0:T(128)} %bitcast.place_ref, bf16[32,64,128]{2,1,0:T(8,128)(2,1)S(1)} %all-to-all-done.held_ref), custom_call_target="tpu_custom_call" | custom-call | tf_op jit(solution)/shard_map/select/pallas_call | solution.py:353
  28.4 49.4 %all_to_all.10.own_ref = bf16[128,96,128]{2,1,0:T(8,128)(2,1)S(1)} all-to-all(bf16[128,96,128]{2,1,0:T(8,128)(2,1)S(1)} %select.11), channel_id=1, replica_groups=mesh['chan'=32,'seg'=4] {'seg','chan'}, dimensions={0} | all-to-all | bytes 6291456 | tf_op jit(solution)/shard_map/all_to_all | solution.py:401
  77.8 0.0 copy-start.1
  77.8 0.2 slice.4
  78.1 1.3 %collective-permute-start = (bf16[128,64,128]{2,1,0:T(8,128)(2,1)S(1)}, bf16[128,64,128]{2,1,0:T(8,128)(2,1)S(1)}, u32[]{:S(2)}, u32[]{:S(2)}) collective-permute-start(bf16[128,64,128]{2,1,0:T(8,128)(2,1)S(1)} %slice.4), channel_id=1, source_target_pairs={{0,1},{1,0},{2,3},{3,2},{4,5},{5,4},{6,7},{7,6},{8,9},{9,8},{10,11... | collective-permute-start | bytes 6291464 | tf_op jit(solution)/shard_map/ppermute | solution.py:402
  79.4 0.0 copy-done.1
  79.4 0.0 copy-start
  79.4 2.4 %near_cross.1.near_ref = bf16[2,32,32,16,128]{4,3,2,1,0:T(8,128)(2,1)S(1)} custom-call(bf16[128,96,128]{2,1,0:T(8,128)(2,1)S(1)} %all_to_all.10.own_ref, bf16[16,256]{1,0:T(8,128)(2,1)S(1)} %copy-done.1), custom_call_target="tpu_custom_call" | custom-call | flops 8589934592 | bytes 11534336 | tf_op jit(solution)/shard_map/near_cross/pallas_call | solution.py:365
  81.7 1.4 %collective-permute-done.other_ref = bf16[128,64,128]{2,1,0:T(8,128)(2,1)S(1)} collective-permute-done((bf16[128,64,128]{2,1,0:T(8,128)(2,1)S(1)}, bf16[128,64,128]{2,1,0:T(8,128)(2,1)S(1)}, u32[]{:S(2)}, u32[]{:S(2)}) %collective-permute-start) | collective-permute-done | bytes 2097184 | tf_op jit(solution)/shard_map/ppermute | solution.py:402
  83.2 0.0 copy-done
  83.2 8.2 %correlate.1 = f32[32,2,128,256]{3,2,1,0:T(8,128)} custom-call(s32[1]{0:T(128)S(6)} %select_n.36.core_ref, bf16[128,96,128]{2,1,0:T(8,128)(2,1)S(1)} %all_to_all.10.own_ref, bf16[128,64,128]{2,1,0:T(8,128)(2,1)S(1)} %collective-permute-done.other_ref, bf16[2,32,32,16,128]{4,3,2,1,0:T(8,128)(2,1)S(1)} %near_cross.1.near_ref, bf16[16,256]{1,0:T(8,128)(2,1)S(1)} %copy-done.1, ...), custom_call_target="tpu_custom_call" | custom-call | tf_op jit(solution)/shard_map/correlate/pallas_call | solution.py:379
  (6 shorter events, 0.1 us)
Async XLA Ops:
  0.0 16.5 %copy-start.3 = (s32[32]{0:T(128)S(1)}, s32[32]{0:T(128)}, u32[]{:S(2)}) copy-start(s32[32]{0:T(128)} %param.10) | copy-start | bytes 388
  0.0 17.0 %copy-start.2 = (s32[32,16]{0,1:T(8,128)S(1)}, s32[32,16]{0,1:T(8,128)}, u32[]{:S(2)}) copy-start(s32[32,16]{0,1:T(8,128)} %param.9) | copy-start | bytes 6148
  0.0 17.3 %copy-start.4 = (s32[64]{0:T(128)S(1)}, s32[64]{0:T(128)}, u32[]{:S(2)}) copy-start(s32[64]{0:T(128)} %param.11) | copy-start | bytes 772
  7.3 19.0 %all-to-all-start = ((bf16[32,64,128]{2,1,0:T(8,128)(2,1)}), bf16[32,64,128]{2,1,0:T(8,128)(2,1)S(1)}, u32[]{:S(2)}, u32[]{:S(2)}) async-start(bf16[32,64,128]{2,1,0:T(8,128)(2,1)} %front.1), calls=%async_computation | async-start | bytes 1048576 | tf_op jit(solution)/shard_map/all_to_all | solution.py:399
  77.8 1.6 %copy-start.1 = (bf16[16,256]{1,0:T(8,128)(2,1)S(1)}, bf16[16,256]{1,0:T(8,128)(2,1)}, u32[]{:S(2)}) copy-start(bf16[16,256]{1,0:T(8,128)(2,1)} %constant.52.clone.mask_ref) | copy-start | bytes 24580
  78.1 5.1 %collective-permute-start = (bf16[128,64,128]{2,1,0:T(8,128)(2,1)S(1)}, bf16[128,64,128]{2,1,0:T(8,128)(2,1)S(1)}, u32[]{:S(2)}, u32[]{:S(2)}) collective-permute-start(bf16[128,64,128]{2,1,0:T(8,128)(2,1)S(1)} %slice.4), channel_id=1, source_target_pairs={{0,1},{1,0},{2,3},{3,2},{4,5},{5,4},{6,7},{7,6},{8,9},{9,8},{10,11... | collective-permute-start | bytes 6291464 | tf_op jit(solution)/shard_map/ppermute | solution.py:402
  79.4 3.8 %copy-start = (bf16[2,256,1024]{2,1,0:T(8,128)(2,1)S(1)}, bf16[2,256,1024]{2,1,0:T(8,128)(2,1)}, u32[]{:S(2)}) copy-start(bf16[2,256,1024]{2,1,0:T(8,128)(2,1)} %constant.53.clone.table_ref) | copy-start | bytes 3145732

commit v6 on v5

--- a/solution.py
+++ b/solution.py
@@ -43,15 +43,15 @@
 
 
 def lag_tables():
-    shifts = (np.arange(LAGS) - LAGS // 2) % SAMPLES
+    shifts = np.arange(LAGS // 2 + 8)
     phase = np.outer(BAND_START + np.arange(FREQS), shifts) % SAMPLES
     angles = phase.astype(np.float32) * np.float32(2.0 * math.pi / SAMPLES)
     norm = 1.0 / math.sqrt(FREQS * SEGS)
     parts = np.stack([np.cos(angles), -np.sin(angles)]).astype(ml_dtypes.bfloat16)
     parts = (parts.astype(np.float32) * norm).astype(ml_dtypes.bfloat16)
-    parts = parts.reshape(2, NBLK // 2, 2, 2, GROUP // 2, LAGS).transpose(5, 3, 1, 0, 2, 4)
-    both = np.stack([parts, parts[:, ::-1]])
-    return both.reshape(2, LAGS, 2 * FREQS)
+    parts = parts.reshape(2, NBLK // 2, 2, 2, GROUP // 2, LAGS // 2 + 8).transpose(0, 5, 3, 1, 2, 4)
+    both = np.stack([parts, parts[:, :, ::-1]])
+    return both.reshape(2, 2, LAGS // 2 + 8, FREQS)
 
 
 def group_mask():
@@ -276,7 +276,7 @@
 
         def cross(pair, carry):
             for part, found in enumerate(cross_of(slot, 0, pair, own_ref, own_ref, mask_ref[...])):
-                cross_ref[slot, :, 2 * pair + part] = found
+                cross_ref[slot, :, NBLK // 2 * part + pair] = found
             return carry
 
         lax.fori_loop(0, NBLK // 2, cross, 0, unroll=UNROLL)
@@ -293,21 +293,42 @@
             for part, found in enumerate(
                 cross_of(slot, 1, pair, other_ref, own_ref, mask_ref[...])
             ):
-                cross_ref[:, 2 * pair + part] = found
+                cross_ref[:, NBLK // 2 * part + pair] = found
             return carry
 
         def lags(pair, carry):
-            sides = []
+            sums = []
+            for part in range(2):
+                tiles = pl.ds(NBLK // 2 * part, NBLK // 2)
+                sides = []
+                for k in range(2):
+                    near = near_ref[slot, 2 * pair + k, tiles].reshape(FREQS // 2, BLOCK)
+                    far = cross_ref[2 * pair + k, tiles].reshape(FREQS // 2, BLOCK)
+                    sides.append(jnp.concatenate([near, far], axis=0))
+                sums.append(
+                    jnp.dot(
+                        table_ref[core, part],
+                        jnp.concatenate(sides, axis=1),
+                        preferred_element_type=jnp.float32,
+                    )
+                )
+            later = (sums[0][:BLOCK] + sums[1][:BLOCK]).T
+            less = sums[0] - sums[1]
+            row = lax.broadcasted_iota(jnp.int32, (8, 2 * BLOCK), 0)
+            back = (8 - row) & 7
+            turned = []
+            for tile in range(15, -1, -1):
+                here, above = less[8 * tile : 8 * tile + 8], less[8 * tile + 8 : 8 * tile + 16]
+                turned.append(
+                    jnp.take_along_axis(
+                        jnp.where(row == 0, above, here), back, axis=0, mode="promise_in_bounds"
+                    )
+                )
+            earlier = jnp.concatenate(turned, axis=0).T
             for k in range(2):
-                near = near_ref[slot, 2 * pair + k].reshape(FREQS, BLOCK)
-                far = cross_ref[2 * pair + k].reshape(FREQS, BLOCK)
-                sides.append(jnp.concatenate([near, far], axis=0))
-            lagged = jnp.dot(
-                table_ref[core], jnp.concatenate(sides, axis=1), preferred_element_type=jnp.float32
-            )
-            both = lagged.T
-            for k in range(2):
-                lag_ref[slot, 2 * pair + k] = both[k * BLOCK : (k + 1) * BLOCK]
+                rows = slice(k * BLOCK, (k + 1) * BLOCK)
+                lag_ref[slot, 2 * pair + k, :, :BLOCK] = earlier[rows]
+                lag_ref[slot, 2 * pair + k, :, BLOCK:] = later[rows]
             return carry
 
         lax.fori_loop(0, NBLK // 2, cross, 0, unroll=UNROLL)

time: 91.9 us -> 89.9 us (0.978)
  Pallas kernels: 20 us -> 18 us
    pallas_call x1, Pallas kernels: 8.25 us -> 6.28 us  [correlate(): pl.pallas_call(correlate_kernel, out_shape=jax.ShapeDtypeStruct((32, SLOT...]
where the time goes in v6:
time: 89.9 us; the launch traced here: 89.6 us
  blocking collectives  49.4 us (55%)
  Pallas kernels  18 us (20%)
  starting transfers between devices  10.5 us (12%)
  waiting for transfers between devices  10.3 us (11%)
    all_to_all x1, blocking collectives, on_device(): lax.all_to_all(sent, ('seg', 'chan'), split_axis=0, concat_axis=0, tiled=...  49.4 us
    all_to_all x1, starting transfers between devices, on_device(): lax.all_to_all(front(traces), 'chan', split_axis=0, concat_axis=0, tiled=...  9.24 us
    all_to_all x1, waiting for transfers between devices, on_device(): lax.all_to_all(front(traces), 'chan', split_axis=0, concat_axis=0, tiled=...  8.93 us
    pallas_call x1, Pallas kernels, front(): pl.pallas_call(front_kernel, out_shape=jax.ShapeDtypeStruct((NBLK, 4 * GR...  7.26 us
    pallas_call x1, Pallas kernels, correlate(): pl.pallas_call(correlate_kernel, out_shape=jax.ShapeDtypeStruct((32, SLOT...  6.28 us
    pallas_call x1, Pallas kernels, near_cross(): pl.pallas_call(near_kernel, out_shape=jax.ShapeDtypeStruct((SLOT_DEV, 32,...  2.35 us
    pallas_call x1, Pallas kernels, select(): pl.pallas_call(select_kernel, out_shape=jax.ShapeDtypeStruct((128, 96, BL...  2.12 us
  transfers between devices with their start and end apart: 2, of which 2 were waited for; matrix products, arithmetic and copies ran while one was open for 1% of the time, Pallas kernels for 3%

profile of v6, /device:TPU:1, one launch (start us, length us, event | category | flops | bytes accessed | tf_op | source)
XLA Modules:
  0.0 89.6 jit_solution(13785116904418387536)
XLA Ops:
  0.0 0.0 copy-start.3
  0.0 0.0 copy-start.2
  0.0 0.0 copy-start.4
  0.0 7.3 %front.1 = bf16[32,64,128]{2,1,0:T(8,128)(2,1)} custom-call(bf16[16384,128]{1,0:T(8,128)(2,1)} %bitcast.7, bf16[8,512,256]{2,1,0:T(8,128)(2,1)} %constant.51.clone.dft_hbm), custom_call_target="tpu_custom_call" | custom-call | tf_op jit(solution)/shard_map/front/pallas_call | solution.py:350
  7.3 9.2 %all-to-all-start = ((bf16[32,64,128]{2,1,0:T(8,128)(2,1)}), bf16[32,64,128]{2,1,0:T(8,128)(2,1)S(1)}, u32[]{:S(2)}, u32[]{:S(2)}) async-start(bf16[32,64,128]{2,1,0:T(8,128)(2,1)} %front.1), calls=%async_computation | async-start | bytes 1048576 | tf_op jit(solution)/shard_map/all_to_all | solution.py:420
  16.5 0.0 copy-done.3
  16.5 0.1 copy.15
  16.6 0.1 reduce-window.9
  16.7 0.1 reduce
  16.8 0.1 convert_reduce_fusion
  16.9 0.1 select_reduce_fusion.3
  17.0 0.0 copy-done.2
  17.0 0.1 copy.16
  17.1 0.1 select_reduce_fusion
  17.3 0.0 copy-done.4
  17.3 0.1 select_reduce_fusion.1
  17.4 8.9 %all-to-all-done.held_ref = bf16[32,64,128]{2,1,0:T(8,128)(2,1)S(1)} async-done(((bf16[32,64,128]{2,1,0:T(8,128)(2,1)}), bf16[32,64,128]{2,1,0:T(8,128)(2,1)S(1)}, u32[]{:S(2)}, u32[]{:S(2)}) %all-to-all-start) | async-done | bytes 524320 | tf_op jit(solution)/shard_map/all_to_all | solution.py:420
  26.3 2.1 %select.11 = bf16[128,96,128]{2,1,0:T(8,128)(2,1)S(1)} custom-call(s32[64]{0:T(128)S(1)} %get-tuple-element.6.first_ref, s32[64]{0:T(128)S(1)} %get-tuple-element.5.second_ref, s32[1]{0:T(128)} %bitcast.place_ref, bf16[32,64,128]{2,1,0:T(8,128)(2,1)S(1)} %all-to-all-done.held_ref), custom_call_target="tpu_custom_call" | custom-call | tf_op jit(solution)/shard_map/select/pallas_call | solution.py:374
  28.4 49.4 %all_to_all.10.own_ref = bf16[128,96,128]{2,1,0:T(8,128)(2,1)S(1)} all-to-all(bf16[128,96,128]{2,1,0:T(8,128)(2,1)S(1)} %select.11), channel_id=1, replica_groups=mesh['chan'=32,'seg'=4] {'seg','chan'}, dimensions={0} | all-to-all | bytes 6291456 | tf_op jit(solution)/shard_map/all_to_all | solution.py:422
  77.8 0.0 copy-start.1
  77.8 0.2 slice.4
  78.1 1.3 %collective-permute-start = (bf16[128,64,128]{2,1,0:T(8,128)(2,1)S(1)}, bf16[128,64,128]{2,1,0:T(8,128)(2,1)S(1)}, u32[]{:S(2)}, u32[]{:S(2)}) collective-permute-start(bf16[128,64,128]{2,1,0:T(8,128)(2,1)S(1)} %slice.4), channel_id=1, source_target_pairs={{0,1},{1,0},{2,3},{3,2},{4,5},{5,4},{6,7},{7,6},{8,9},{9,8},{10,11... | collective-permute-start | bytes 6291464 | tf_op jit(solution)/shard_map/ppermute | solution.py:423
  79.4 0.0 copy-done.1
  79.4 0.0 copy-start
  79.4 2.4 %near_cross.1.near_ref = bf16[2,32,32,16,128]{4,3,2,1,0:T(8,128)(2,1)S(1)} custom-call(bf16[128,96,128]{2,1,0:T(8,128)(2,1)S(1)} %all_to_all.10.own_ref, bf16[16,256]{1,0:T(8,128)(2,1)S(1)} %copy-done.1), custom_call_target="tpu_custom_call" | custom-call | flops 8589934592 | bytes 11534336 | tf_op jit(solution)/shard_map/near_cross/pallas_call | solution.py:386
  81.7 1.4 %collective-permute-done.other_ref = bf16[128,64,128]{2,1,0:T(8,128)(2,1)S(1)} collective-permute-done((bf16[128,64,128]{2,1,0:T(8,128)(2,1)S(1)}, bf16[128,64,128]{2,1,0:T(8,128)(2,1)S(1)}, u32[]{:S(2)}, u32[]{:S(2)}) %collective-permute-start) | collective-permute-done | bytes 2097184 | tf_op jit(solution)/shard_map/ppermute | solution.py:423
  83.2 0.0 copy-done
  83.2 6.3 %correlate.1 = f32[32,2,128,256]{3,2,1,0:T(8,128)} custom-call(s32[1]{0:T(128)S(6)} %select_n.36.core_ref, bf16[128,96,128]{2,1,0:T(8,128)(2,1)S(1)} %all_to_all.10.own_ref, bf16[128,64,128]{2,1,0:T(8,128)(2,1)S(1)} %collective-permute-done.other_ref, bf16[2,32,32,16,128]{4,3,2,1,0:T(8,128)(2,1)S(1)} %near_cross.1.near_ref, bf16[16,256]{1,0:T(8,128)(2,1)S(1)} %copy-done.1, ...), custom_call_target="tpu_custom_call" | custom-call | tf_op jit(solution)/shard_map/correlate/pallas_call | solution.py:400
  (6 shorter events, 0.1 us)
Async XLA Ops:
  0.0 16.5 %copy-start.3 = (s32[32]{0:T(128)S(1)}, s32[32]{0:T(128)}, u32[]{:S(2)}) copy-start(s32[32]{0:T(128)} %param.10) | copy-start | bytes 388
  0.0 17.0 %copy-start.2 = (s32[32,16]{0,1:T(8,128)S(1)}, s32[32,16]{0,1:T(8,128)}, u32[]{:S(2)}) copy-start(s32[32,16]{0,1:T(8,128)} %param.9) | copy-start | bytes 6148
  0.0 17.3 %copy-start.4 = (s32[64]{0:T(128)S(1)}, s32[64]{0:T(128)}, u32[]{:S(2)}) copy-start(s32[64]{0:T(128)} %param.11) | copy-start | bytes 772
  7.3 19.0 %all-to-all-start = ((bf16[32,64,128]{2,1,0:T(8,128)(2,1)}), bf16[32,64,128]{2,1,0:T(8,128)(2,1)S(1)}, u32[]{:S(2)}, u32[]{:S(2)}) async-start(bf16[32,64,128]{2,1,0:T(8,128)(2,1)} %front.1), calls=%async_computation | async-start | bytes 1048576 | tf_op jit(solution)/shard_map/all_to_all | solution.py:420
  77.8 1.6 %copy-start.1 = (bf16[16,256]{1,0:T(8,128)(2,1)S(1)}, bf16[16,256]{1,0:T(8,128)(2,1)}, u32[]{:S(2)}) copy-start(bf16[16,256]{1,0:T(8,128)(2,1)} %constant.52.clone.mask_ref) | copy-start | bytes 24580
  78.1 5.1 %collective-permute-start = (bf16[128,64,128]{2,1,0:T(8,128)(2,1)S(1)}, bf16[128,64,128]{2,1,0:T(8,128)(2,1)S(1)}, u32[]{:S(2)}, u32[]{:S(2)}) collective-permute-start(bf16[128,64,128]{2,1,0:T(8,128)(2,1)S(1)} %slice.4), channel_id=1, source_target_pairs={{0,1},{1,0},{2,3},{3,2},{4,5},{5,4},{6,7},{7,6},{8,9},{9,8},{10,11... | collective-permute-start | bytes 6291464 | tf_op jit(solution)/shard_map/ppermute | solution.py:423
  79.4 3.8 %copy-start = (bf16[2,2,136,512]{3,2,1,0:T(8,128)(2,1)S(1)}, bf16[2,2,136,512]{3,2,1,0:T(8,128)(2,1)}, u32[]{:S(2)}) copy-start(bf16[2,2,136,512]{3,2,1,0:T(8,128)(2,1)} %constant.53.clone.table_ref) | copy-start | bytes 1671172

commit v7 on v3

--- a/solution.py
+++ b/solution.py
@@ -43,21 +43,18 @@
 
 
 def lag_tables():
-    shifts = (np.arange(LAGS) - LAGS // 2) % SAMPLES
+    shifts = np.arange(LAGS // 2 + 8)
     phase = np.outer(BAND_START + np.arange(FREQS), shifts) % SAMPLES
     angles = phase.astype(np.float32) * np.float32(2.0 * math.pi / SAMPLES)
     norm = 1.0 / math.sqrt(FREQS * SEGS)
     parts = np.stack([np.cos(angles), -np.sin(angles)]).astype(ml_dtypes.bfloat16)
     parts = (parts.astype(np.float32) * norm).astype(ml_dtypes.bfloat16)
-    parts = parts.reshape(2, FREQS // GROUP, 2, GROUP // 2, LAGS).transpose(4, 1, 0, 2, 3)
-    both = np.stack([parts, parts[:, :, :, ::-1]])
-    return both.reshape(2, LAGS, 2 * FREQS)
+    return parts.transpose(0, 2, 1)
 
 
 def group_mask():
-    lane = np.arange(256)
-    own = (lane // 16 % 2) * 8 + lane % 8
-    return (np.arange(GROUP)[:, None] == own[None, :]).astype(ml_dtypes.bfloat16)
+    lane, row = np.arange(256)[None, :], np.arange(GROUP)[:, None]
+    return (lane // 16 % 2 * 8 + lane % 8 == row).astype(ml_dtypes.bfloat16)
 
 
 def pair_blocks(pair_offsets, pair_counts, pair_owner, block_count, slot_count):
@@ -208,96 +205,101 @@
 
 def select_kernel(first_ref, second_ref, place_ref, held_ref, out_ref, rows_ref):
     lane = lax.broadcasted_iota(jnp.int32, (32, BLOCK), 1)
-    left = (lane < 64) == (place_ref[0] % 2 == 0)
+    left = (lane < 64) == ((place_ref[0] & 1) == 0)
 
     def turn(block, carry):
         tiles = held_ref[block].astype(jnp.float32)
-        for core in range(2):
-            order = tiles if core == 0 else jnp.concatenate(
-                [tiles[16:32], tiles[0:16], tiles[48:64], tiles[32:48]], axis=0
-            )
-            twice = jnp.concatenate([order, order], axis=0)
-            rows_ref[core, block] = twice.T.astype(jnp.bfloat16)
-        return carry
-
-    lax.fori_loop(0, NBLK, turn, 0, unroll=8)
+        rows_ref[block] = jnp.concatenate([tiles, tiles], axis=0).T.astype(jnp.bfloat16)
+        return carry
+
+    lax.fori_loop(0, NBLK, turn, 0, unroll=True)
 
     def send(chan, carry):
         slots = [SLOT_DEV * chan + slot for slot in range(SLOT_DEV)]
         for seg in range(4):
-            core = seg % 2
-            dest = 4 * chan + seg
-            for slot in range(SLOT_DEV):
-                second = second_ref[slots[slot]]
-                for part in range(2):
-                    out_ref[dest, pl.ds(32 * slot + 16 * part, 16), :] = held_ref[
-                        second, pl.ds(32 * part + 16 * core, 16), :
-                    ]
-            one = rows_ref[core, first_ref[slots[0]], pl.ds(32 * seg, 32), :]
-            two = rows_ref[core, first_ref[slots[1]], pl.ds(32 * seg, 32), :]
+            dest = NBLK * seg + chan
+            out_ref[dest, pl.ds(0, 64), :] = held_ref[second_ref[slots[seg % 2]]]
+            one = rows_ref[first_ref[slots[0]], pl.ds(32 * seg, 32), :]
+            two = rows_ref[first_ref[slots[1]], pl.ds(32 * seg, 32), :]
             out_ref[dest, pl.ds(64, 32), :] = jnp.where(left, one, two)
         return carry
 
-    lax.fori_loop(0, NBLK, send, 0, unroll=8)
+    lax.fori_loop(0, NBLK, send, 0, unroll=True)
 
 
 def correlate_kernel(
-    core_ref, own_ref, other_ref, mask_ref, table_ref, out_hbm, cross_ref, lag_ref, out_sem
+    slot_ref, second_ref, own_ref, mask_ref, table_ref, filled_hbm, out_hbm, cross_ref, lag_ref, out_sem
 ):
-    core = core_ref[0]
+    del filled_hbm
+    slot = slot_ref[0]
+
+    def cross(group, carry):
+        left = lax.broadcasted_iota(jnp.int32, (32, BLOCK), 1) < 64
+        upper = []
+        lower = []
+        lanes = []
+        for seg in range(4):
+            src = NBLK * (seg ^ slot) + group
+            real, imag = second_ref[src, pl.ds(0, 32), :], second_ref[src, pl.ds(32, 32), :]
+            upper += [real, imag]
+            lower += [-imag, real]
+            lanes.append(own_ref[src, pl.ds(64, 32), :])
+        second = jnp.concatenate(
+            [jnp.concatenate(upper, axis=0), jnp.concatenate(lower, axis=0)], axis=1
+        )
+        first = jnp.concatenate(
+            [jnp.where(left, lanes[0], lanes[1]), jnp.where(left, lanes[2], lanes[3])], axis=1
+        )
+        mask = mask_ref[...]
+        spread = [jnp.broadcast_to(first[i : i + 1], (GROUP, 256)) * mask for i in range(32)]
+        found = jnp.dot(
+            jnp.concatenate(spread, axis=0), second, preferred_element_type=jnp.float32
+        ).astype(jnp.bfloat16)
+        for part in range(2):
+            cross_ref[:, NBLK * part + group] = found[:, part * BLOCK : (part + 1) * BLOCK].reshape(
+                32, GROUP, BLOCK
+            )
+        return carry
+
+    def lags(pair, carry):
+        sums = []
+        for part in range(2):
+            tiles = pl.ds(NBLK * part, NBLK)
+            sides = [cross_ref[2 * pair + k, tiles].reshape(FREQS, BLOCK) for k in range(2)]
+            sums.append(
+                jnp.dot(
+                    table_ref[part],
+                    jnp.concatenate(sides, axis=1),
+                    preferred_element_type=jnp.float32,
+                )
+            )
+        later = (sums[0][:BLOCK] + sums[1][:BLOCK]).T
+        less = sums[0] - sums[1]
+        row = lax.broadcasted_iota(jnp.int32, (8, 2 * BLOCK), 0)
+        back = (8 - row) & 7
+        turned = []
+        for tile in range(15, -1, -1):
+            here, above = less[8 * tile : 8 * tile + 8], less[8 * tile + 8 : 8 * tile + 16]
+            turned.append(
+                jnp.take_along_axis(
+                    jnp.where(row == 0, above, here), back, axis=0, mode="promise_in_bounds"
+                )
+            )
+        earlier = jnp.concatenate(turned, axis=0).T
+        for k in range(2):
+            rows = slice(k * BLOCK, (k + 1) * BLOCK)
+            lag_ref[2 * pair + k, :, :BLOCK] = earlier[rows]
+            lag_ref[2 * pair + k, :, BLOCK:] = later[rows]
+        return carry
+
     leaving = []
-    for slot in range(SLOT_DEV):
-
-        def cross(group, carry):
-            order = [slot, 1 - slot, 2 + slot, 3 - slot]
-            upper = []
-            lower = []
-            for seg in order:
-                src = 4 * group + seg
-                tiles = []
-                for part in range(2):
-                    rows = pl.ds(32 * slot + 16 * part, 16)
-                    tiles.append([own_ref[src, rows, :], other_ref[src, rows, :]])
-                upper += tiles[0] + tiles[1]
-                lower += [-tiles[1][0], -tiles[1][1]] + tiles[0]
-            second = jnp.concatenate(
-                [jnp.concatenate(upper, axis=0), jnp.concatenate(lower, axis=0)], axis=1
-            )
-            lane = lax.broadcasted_iota(jnp.int32, (32, BLOCK), 1)
-            left = (lane < 64) == (slot == 0)
-            lanes = [own_ref[4 * group + seg, pl.ds(64, 32), :] for seg in range(4)]
-            first = jnp.concatenate(
-                [jnp.where(left, lanes[0], lanes[1]), jnp.where(left, lanes[2], lanes[3])], axis=1
-            )
-            mask = mask_ref[...]
-            spread = [jnp.broadcast_to(first[i : i + 1], (GROUP, 256)) * mask for i in range(32)]
-            found = jnp.dot(
-                jnp.concatenate(spread, axis=0), second, preferred_element_type=jnp.float32
-            ).astype(jnp.bfloat16)
-            for part in range(2):
-                cross_ref[:, 2 * group + part] = found[
-                    :, part * BLOCK : (part + 1) * BLOCK
-                ].reshape(32, GROUP, BLOCK)
-            return carry
-
-        def lags(pair, carry):
-            sides = [cross_ref[2 * pair + k].reshape(2 * FREQS, BLOCK) for k in range(2)]
-            lagged = jnp.dot(
-                table_ref[core], jnp.concatenate(sides, axis=1), preferred_element_type=jnp.float32
-            )
-            for k in range(2):
-                lag_ref[slot, 2 * pair + k] = lagged[:, k * BLOCK : (k + 1) * BLOCK].T
-            return carry
-
-        lax.fori_loop(0, NBLK, cross, 0, unroll=UNROLL)
-        for step in range(16 // PAIRS):
-            lax.fori_loop(PAIRS * step, PAIRS * (step + 1), lags, 0, unroll=True)
-            rows = pl.ds(2 * PAIRS * step, 2 * PAIRS)
-            copy = pltpu.make_async_copy(
-                lag_ref.at[slot, rows], out_hbm.at[rows, slot], out_sem.at[slot, step]
-            )
-            copy.start()
-            leaving.append(copy)
+    lax.fori_loop(0, NBLK, cross, 0, unroll=UNROLL)
+    for step in range(16 // PAIRS):
+        lax.fori_loop(PAIRS * step, PAIRS * (step + 1), lags, 0, unroll=True)
+        rows = pl.ds(2 * PAIRS * step, 2 * PAIRS)
+        copy = pltpu.make_async_copy(lag_ref.at[rows], out_hbm.at[rows, slot], out_sem.at[step])
+        copy.start()
+        leaving.append(copy)
     for copy in leaving:
         copy.wait()
 
@@ -333,27 +335,44 @@
         select_kernel,
         out_shape=jax.ShapeDtypeStruct((128, 96, BLOCK), jnp.bfloat16),
         in_specs=[smem, smem, smem, pl.BlockSpec(memory_space=pltpu.VMEM)],
-        scratch_shapes=[pltpu.VMEM((2, NBLK, BLOCK, BLOCK), jnp.bfloat16)],
+        scratch_shapes=[pltpu.VMEM((NBLK, BLOCK, BLOCK), jnp.bfloat16)],
         compiler_params=pltpu.CompilerParams(vmem_limit_bytes=VMEM),
         name="select",
     )(slot_first, slot_second, place, held)
 
 
+def correlate_slot(slot, second, own, filled=None):
+    hbm = pl.BlockSpec(memory_space=pl.ANY)
+    vmem = pl.BlockSpec(memory_space=pltpu.VMEM)
+    kernel = correlate_kernel
+    operands = [slot, second, own, jnp.asarray(group_mask()), jnp.asarray(lag_tables())]
+    specs = [pl.BlockSpec(memory_space=pltpu.SMEM)] + [vmem] * 4
+    aliases = {}
+    if filled is None:
+        kernel = lambda *refs: correlate_kernel(*refs[:5], None, *refs[5:])
+    else:
+        operands.append(filled)
+        specs.append(hbm)
+        aliases = {5: 0}
+    return pl.pallas_call(
+        kernel,
+        out_shape=jax.ShapeDtypeStruct((32, SLOT_DEV, BLOCK, LAGS), jnp.float32),
+        in_specs=specs,
+        out_specs=hbm,
+        scratch_shapes=[
+            pltpu.VMEM((32, 2 * NBLK, GROUP, BLOCK), jnp.bfloat16),
+            pltpu.VMEM((32, BLOCK, LAGS), jnp.float32),
+            pltpu.SemaphoreType.DMA((16 // PAIRS,)),
+        ],
+        input_output_aliases=aliases,
+        compiler_params=pltpu.CompilerParams(vmem_limit_bytes=24 * 1024 * 1024),
+        cost_estimate=pl.CostEstimate(flops=8 << 30, transcendentals=0, bytes_accessed=9 << 20),
+        name="correlate_first" if filled is None else "correlate_second",
+    )(*operands)
+
+
 def correlate(core, own, other):
-    vmem = pl.BlockSpec(memory_space=pltpu.VMEM)
-    return pl.pallas_call(
-        correlate_kernel,
-        out_shape=jax.ShapeDtypeStruct((32, SLOT_DEV, BLOCK, LAGS), jnp.float32),
-        in_specs=[pl.BlockSpec(memory_space=pltpu.SMEM), vmem, vmem, vmem, vmem],
-        out_specs=pl.BlockSpec(memory_space=pl.ANY),
-        scratch_shapes=[
-            pltpu.VMEM((32, 2 * FREQS // GROUP, GROUP, BLOCK), jnp.bfloat16),
-            pltpu.VMEM((SLOT_DEV, 32, BLOCK, LAGS), jnp.float32),
-            pltpu.SemaphoreType.DMA((SLOT_DEV, 16 // PAIRS)),
-        ],
-        compiler_params=pltpu.CompilerParams(vmem_limit_bytes=VMEM),
-        name="correlate",
-    )(core, own, other, jnp.asarray(group_mask()), jnp.asarray(lag_tables()))
+    return correlate_slot(1 - core, other, own, correlate_slot(core, own, own))
 
 
 def on_device(traces, pair_offsets, pair_counts, pair_owner):
@@ -363,7 +382,7 @@
     seg = lax.axis_index("seg").astype(jnp.int32).reshape(1)
     held = lax.all_to_all(front(traces), "chan", split_axis=0, concat_axis=0, tiled=True)
     sent = select(slot_first, slot_second, seg, held)
-    own = lax.all_to_all(sent, ("chan", "seg"), split_axis=0, concat_axis=0, tiled=True)
+    own = lax.all_to_all(sent, ("seg", "chan"), split_axis=0, concat_axis=0, tiled=True)
     other = lax.ppermute(own[:, :64], "seg", [(0, 1), (1, 0), (2, 3), (3, 2)])
     return correlate(seg % 2, own, other)
 

time: 94.2 us -> 88.8 us (0.943)
  waiting for transfers between devices: 13.1 us -> 8.93 us
  Pallas kernels: 19.8 us -> 18.4 us
  starting transfers between devices: 9.5 us -> 10.5 us
    ppermute x1, waiting for transfers between devices: 4.14 us -> 0.01 us  [on_device(): other = lax.ppermute(own[:, :64], 'seg', [(0, 1), (1, 0), (2, 3), (3, 2)])]
    ppermute x1, starting transfers between devices: 0.27 us -> 1.3 us  [on_device(): other = lax.ppermute(own[:, :64], 'seg', [(0, 1), (1, 0), (2, 3), (3, 2)])]
    pallas_call x1 -> x2, Pallas kernels: 10.6 us -> 9.84 us  [correlate_slot(): pl.pallas_call(kernel, out_shape=jax.ShapeDtypeStruct((32, SLOT_DEV, BLOC...]
  transfers between devices with their start and end apart: 2 -> 2, of which waited for: 2 -> 1; matrix products, arithmetic and copies ran while one was open for 1% -> 1% of each run, Pallas kernels for 0% -> 6%
where the time goes in v7:
time: 88.8 us; the launch traced here: 88.6 us
  blocking collectives  49.4 us (56%)
  Pallas kernels  18.4 us (21%)
  starting transfers between devices  10.5 us (12%)
  waiting for transfers between devices  8.93 us (10%)
    all_to_all x1, blocking collectives, on_device(): lax.all_to_all(sent, ('seg', 'chan'), split_axis=0, concat_axis=0, tiled=...  49.4 us
    pallas_call x2, Pallas kernels, correlate_slot(): pl.pallas_call(kernel, out_shape=jax.ShapeDtypeStruct((32, SLOT_DEV, BLOC...  9.84 us
    all_to_all x1, starting transfers between devices, on_device(): lax.all_to_all(front(traces), 'chan', split_axis=0, concat_axis=0, tiled=...  9.24 us
    all_to_all x1, waiting for transfers between devices, on_device(): lax.all_to_all(front(traces), 'chan', split_axis=0, concat_axis=0, tiled=...  8.93 us
    pallas_call x1, Pallas kernels, front(): pl.pallas_call(front_kernel, out_shape=jax.ShapeDtypeStruct((NBLK, 4 * GR...  7.26 us
  transfers between devices with their start and end apart: 2, of which 1 were waited for; matrix products, arithmetic and copies ran while one was open for 1% of the time, Pallas kernels for 6%

profile of v7, /device:TPU:1, one launch (start us, length us, event | category | flops | bytes accessed | tf_op | source)
XLA Modules:
  0.0 88.6 jit_solution(1330725851210099706)
XLA Ops:
  0.0 0.0 copy-start.3
  0.0 0.0 copy-start.2
  0.0 0.0 copy-start.4
  0.0 7.3 %front.1 = bf16[32,64,128]{2,1,0:T(8,128)(2,1)} custom-call(bf16[16384,128]{1,0:T(8,128)(2,1)} %bitcast.7, bf16[8,512,256]{2,1,0:T(8,128)(2,1)} %constant.52.clone.dft_hbm), custom_call_target="tpu_custom_call" | custom-call | tf_op jit(solution)/shard_map/front/pallas_call | solution.py:310
  7.3 9.2 %all-to-all-start = ((bf16[32,64,128]{2,1,0:T(8,128)(2,1)}), bf16[32,64,128]{2,1,0:T(8,128)(2,1)S(1)}, u32[]{:S(2)}, u32[]{:S(2)}) async-start(bf16[32,64,128]{2,1,0:T(8,128)(2,1)} %front.1), calls=%async_computation | async-start | bytes 1048576 | tf_op jit(solution)/shard_map/all_to_all | solution.py:383
  16.5 0.0 copy-done.3
  16.5 0.1 copy.17
  16.6 0.1 reduce-window.9
  16.7 0.1 reduce
  16.8 0.1 convert_reduce_fusion
  16.9 0.1 select_reduce_fusion.3
  17.0 0.0 copy-done.2
  17.0 0.1 copy.18
  17.1 0.1 select_reduce_fusion
  17.3 0.0 copy-done.4
  17.3 0.1 select_reduce_fusion.1
  17.4 8.9 %all-to-all-done.held_ref = bf16[32,64,128]{2,1,0:T(8,128)(2,1)S(1)} async-done(((bf16[32,64,128]{2,1,0:T(8,128)(2,1)}), bf16[32,64,128]{2,1,0:T(8,128)(2,1)S(1)}, u32[]{:S(2)}, u32[]{:S(2)}) %all-to-all-start) | async-done | bytes 524320 | tf_op jit(solution)/shard_map/all_to_all | solution.py:383
  26.3 1.3 %select.11 = bf16[128,96,128]{2,1,0:T(8,128)(2,1)S(1)} custom-call(s32[64]{0:T(128)S(1)} %get-tuple-element.6.first_ref, s32[64]{0:T(128)S(1)} %get-tuple-element.5.second_ref, s32[1]{0:T(128)} %bitcast.place_ref, bf16[32,64,128]{2,1,0:T(8,128)(2,1)S(1)} %all-to-all-done.held_ref), custom_call_target="tpu_custom_call" | custom-call | tf_op jit(solution)/shard_map/select/pallas_call | solution.py:334
  27.6 49.4 %all_to_all.10.refs_1_.refs_2_.own_ref = bf16[128,96,128]{2,1,0:T(8,128)(2,1)S(1)} all-to-all(bf16[128,96,128]{2,1,0:T(8,128)(2,1)S(1)} %select.11), channel_id=1, replica_groups=mesh['chan'=32,'seg'=4] {'seg','chan'}, dimensions={0} | all-to-all | bytes 6291456 | tf_op jit(solution)/shard_map/all_to_all | solution.py:385
  77.0 0.0 copy-start
  77.0 0.0 copy-start.1
  77.0 0.2 slice.4
  77.3 1.3 %collective-permute-start = (bf16[128,64,128]{2,1,0:T(8,128)(2,1)S(1)}, bf16[128,64,128]{2,1,0:T(8,128)(2,1)S(1)}, u32[]{:S(2)}, u32[]{:S(2)}) collective-permute-start(bf16[128,64,128]{2,1,0:T(8,128)(2,1)S(1)} %slice.4), channel_id=1, source_target_pairs={{0,1},{1,0},{2,3},{3,2},{4,5},{5,4},{6,7},{7,6},{8,9},{9,8},{10,11... | collective-permute-start | bytes 6291464 | tf_op jit(solution)/shard_map/ppermute | solution.py:386
  78.6 0.0 copy-done
  78.6 0.0 copy-done.1
  78.6 4.9 %correlate_first.1.filled_hbm = f32[32,2,128,256]{3,2,1,0:T(8,128)} custom-call(s32[1]{0:T(128)S(6)} %select_n.36.refs_0_, bf16[128,96,128]{2,1,0:T(8,128)(2,1)S(1)} %all_to_all.10.refs_1_.refs_2_.own_ref, bf16[128,96,128]{2,1,0:T(8,128)(2,1)S(1)} %all_to_all.10.refs_1_.refs_2_.own_ref, bf16[16,256]{1,0:T(8,128)(2,1)S(1)} %copy-done.1, ...), custom_call_target="tpu_custom_call" | custom-call | flops 8589934592 | bytes 9437184 | tf_op jit(solution)/shard_map/correlate_first/pallas_call | solution.py:357
  83.5 0.0 collective-permute-done.second_ref
  83.5 4.9 %correlate_second.1 = f32[32,2,128,256]{3,2,1,0:T(8,128)} custom-call(s32[1]{0:T(128)S(6)} %sub.17.slot_ref, bf16[128,64,128]{2,1,0:T(8,128)(2,1)S(1)} %collective-permute-done.second_ref, bf16[128,96,128]{2,1,0:T(8,128)(2,1)S(1)} %all_to_all.10.refs_1_.refs_2_.own_ref, bf16[16,256]{1,0:T(8,128)(2,1)S(1)} %copy-done.1, ...), custom_call_target="tpu_custom_call", output_to_operand_aliasing={{}: (5, {})} | custom-call | flops 8589934592 | bytes 9437184 | tf_op jit(solution)/shard_map/correlate_second/pallas_call | solution.py:357
  (6 shorter events, 0.1 us)
Async XLA Ops:
  0.0 16.5 %copy-start.3 = (s32[32]{0:T(128)S(1)}, s32[32]{0:T(128)}, u32[]{:S(2)}) copy-start(s32[32]{0:T(128)} %param.11) | copy-start | bytes 388
  0.0 17.0 %copy-start.2 = (s32[32,16]{0,1:T(8,128)S(1)}, s32[32,16]{0,1:T(8,128)}, u32[]{:S(2)}) copy-start(s32[32,16]{0,1:T(8,128)} %param.10) | copy-start | bytes 6148
  0.0 17.3 %copy-start.4 = (s32[64]{0:T(128)S(1)}, s32[64]{0:T(128)}, u32[]{:S(2)}) copy-start(s32[64]{0:T(128)} %param.12) | copy-start | bytes 772
  7.3 19.0 %all-to-all-start = ((bf16[32,64,128]{2,1,0:T(8,128)(2,1)}), bf16[32,64,128]{2,1,0:T(8,128)(2,1)S(1)}, u32[]{:S(2)}, u32[]{:S(2)}) async-start(bf16[32,64,128]{2,1,0:T(8,128)(2,1)} %front.1), calls=%async_computation | async-start | bytes 1048576 | tf_op jit(solution)/shard_map/all_to_all | solution.py:383
  77.0 1.6 %copy-start = (bf16[2,136,512]{2,1,0:T(8,128)(2,1)S(1)}, bf16[2,136,512]{2,1,0:T(8,128)(2,1)}, u32[]{:S(2)}) copy-start(bf16[2,136,512]{2,1,0:T(8,128)(2,1)} %constant.54.clone.refs_4_.table_ref) | copy-start | bytes 835588
  77.0 1.6 %copy-start.1 = (bf16[16,256]{1,0:T(8,128)(2,1)S(1)}, bf16[16,256]{1,0:T(8,128)(2,1)}, u32[]{:S(2)}) copy-start(bf16[16,256]{1,0:T(8,128)(2,1)} %constant.53.clone.refs_3_.mask_ref) | copy-start | bytes 24580
  77.3 6.2 %collective-permute-start = (bf16[128,64,128]{2,1,0:T(8,128)(2,1)S(1)}, bf16[128,64,128]{2,1,0:T(8,128)(2,1)S(1)}, u32[]{:S(2)}, u32[]{:S(2)}) collective-permute-start(bf16[128,64,128]{2,1,0:T(8,128)(2,1)S(1)} %slice.4), channel_id=1, source_target_pairs={{0,1},{1,0},{2,3},{3,2},{4,5},{5,4},{6,7},{7,6},{8,9},{9,8},{10,11... | collective-permute-start | bytes 6291464 | tf_op jit(solution)/shard_map/ppermute | solution.py:386

commit v8 on v7

--- a/solution.py
+++ b/solution.py
@@ -21,7 +21,7 @@
 GROUP = 16
 RADIX = 16
 VMEM = 32 * 1024 * 1024
-PAIRS = 4
+PAIRS = 2
 UNROLL = 32
 FETCHES = 8
 

time: 88.8 us -> 88.5 us (level)
  transfers between devices with their start and end apart: 2 -> 2, of which waited for: 1 -> 1; matrix products, arithmetic and copies ran while one was open for 1% -> 1% of each run, Pallas kernels for 6% -> 5%
where the time goes in v8:
time: 88.5 us; the launch traced here: 88.3 us
  blocking collectives  49.4 us (56%)
  Pallas kernels  18.1 us (20%)
  starting transfers between devices  10.5 us (12%)
  waiting for transfers between devices  8.93 us (10%)
    all_to_all x1, blocking collectives, on_device(): lax.all_to_all(sent, ('seg', 'chan'), split_axis=0, concat_axis=0, tiled=...  49.4 us
    pallas_call x2, Pallas kernels, correlate_slot(): pl.pallas_call(kernel, out_shape=jax.ShapeDtypeStruct((32, SLOT_DEV, BLOC...  9.55 us
    all_to_all x1, starting transfers between devices, on_device(): lax.all_to_all(front(traces), 'chan', split_axis=0, concat_axis=0, tiled=...  9.24 us
    all_to_all x1, waiting for transfers between devices, on_device(): lax.all_to_all(front(traces), 'chan', split_axis=0, concat_axis=0, tiled=...  8.93 us
    pallas_call x1, Pallas kernels, front(): pl.pallas_call(front_kernel, out_shape=jax.ShapeDtypeStruct((NBLK, 4 * GR...  7.26 us
  transfers between devices with their start and end apart: 2, of which 1 were waited for; matrix products, arithmetic and copies ran while one was open for 1% of the time, Pallas kernels for 5%

profile of v8, /device:TPU:1, one launch (start us, length us, event | category | flops | bytes accessed | tf_op | source)
XLA Modules:
  0.0 88.3 jit_solution(13562136657617290193)
XLA Ops:
  0.0 0.0 copy-start.3
  0.0 0.0 copy-start.2
  0.0 0.0 copy-start.4
  0.0 7.3 %front.1 = bf16[32,64,128]{2,1,0:T(8,128)(2,1)} custom-call(bf16[16384,128]{1,0:T(8,128)(2,1)} %bitcast.7, bf16[8,512,256]{2,1,0:T(8,128)(2,1)} %constant.52.clone.dft_hbm), custom_call_target="tpu_custom_call" | custom-call | tf_op jit(solution)/shard_map/front/pallas_call | solution.py:310
  7.3 9.2 %all-to-all-start = ((bf16[32,64,128]{2,1,0:T(8,128)(2,1)}), bf16[32,64,128]{2,1,0:T(8,128)(2,1)S(1)}, u32[]{:S(2)}, u32[]{:S(2)}) async-start(bf16[32,64,128]{2,1,0:T(8,128)(2,1)} %front.1), calls=%async_computation | async-start | bytes 1048576 | tf_op jit(solution)/shard_map/all_to_all | solution.py:383
  16.5 0.0 copy-done.3
  16.5 0.1 copy.17
  16.6 0.1 reduce-window.9
  16.7 0.1 reduce
  16.8 0.1 convert_reduce_fusion
  16.9 0.1 select_reduce_fusion.3
  17.0 0.0 copy-done.2
  17.0 0.1 copy.18
  17.1 0.1 select_reduce_fusion
  17.3 0.0 copy-done.4
  17.3 0.1 select_reduce_fusion.1
  17.4 8.9 %all-to-all-done.held_ref = bf16[32,64,128]{2,1,0:T(8,128)(2,1)S(1)} async-done(((bf16[32,64,128]{2,1,0:T(8,128)(2,1)}), bf16[32,64,128]{2,1,0:T(8,128)(2,1)S(1)}, u32[]{:S(2)}, u32[]{:S(2)}) %all-to-all-start) | async-done | bytes 524320 | tf_op jit(solution)/shard_map/all_to_all | solution.py:383
  26.3 1.3 %select.11 = bf16[128,96,128]{2,1,0:T(8,128)(2,1)S(1)} custom-call(s32[64]{0:T(128)S(1)} %get-tuple-element.6.first_ref, s32[64]{0:T(128)S(1)} %get-tuple-element.5.second_ref, s32[1]{0:T(128)} %bitcast.place_ref, bf16[32,64,128]{2,1,0:T(8,128)(2,1)S(1)} %all-to-all-done.held_ref), custom_call_target="tpu_custom_call" | custom-call | tf_op jit(solution)/shard_map/select/pallas_call | solution.py:334
  27.6 49.4 %all_to_all.10.refs_1_.refs_2_.own_ref = bf16[128,96,128]{2,1,0:T(8,128)(2,1)S(1)} all-to-all(bf16[128,96,128]{2,1,0:T(8,128)(2,1)S(1)} %select.11), channel_id=1, replica_groups=mesh['chan'=32,'seg'=4] {'seg','chan'}, dimensions={0} | all-to-all | bytes 6291456 | tf_op jit(solution)/shard_map/all_to_all | solution.py:385
  77.0 0.0 copy-start
  77.0 0.0 copy-start.1
  77.0 0.2 slice.4
  77.3 1.3 %collective-permute-start = (bf16[128,64,128]{2,1,0:T(8,128)(2,1)S(1)}, bf16[128,64,128]{2,1,0:T(8,128)(2,1)S(1)}, u32[]{:S(2)}, u32[]{:S(2)}) collective-permute-start(bf16[128,64,128]{2,1,0:T(8,128)(2,1)S(1)} %slice.4), channel_id=1, source_target_pairs={{0,1},{1,0},{2,3},{3,2},{4,5},{5,4},{6,7},{7,6},{8,9},{9,8},{10,11... | collective-permute-start | bytes 6291464 | tf_op jit(solution)/shard_map/ppermute | solution.py:386
  78.6 0.0 copy-done
  78.6 0.0 copy-done.1
  78.6 4.8 %correlate_first.1.filled_hbm = f32[32,2,128,256]{3,2,1,0:T(8,128)} custom-call(s32[1]{0:T(128)S(6)} %select_n.36.refs_0_, bf16[128,96,128]{2,1,0:T(8,128)(2,1)S(1)} %all_to_all.10.refs_1_.refs_2_.own_ref, bf16[128,96,128]{2,1,0:T(8,128)(2,1)S(1)} %all_to_all.10.refs_1_.refs_2_.own_ref, bf16[16,256]{1,0:T(8,128)(2,1)S(1)} %copy-done.1, ...), custom_call_target="tpu_custom_call" | custom-call | flops 8589934592 | bytes 9437184 | tf_op jit(solution)/shard_map/correlate_first/pallas_call | solution.py:357
  83.4 0.0 collective-permute-done.second_ref
  83.4 4.8 %correlate_second.1 = f32[32,2,128,256]{3,2,1,0:T(8,128)} custom-call(s32[1]{0:T(128)S(6)} %sub.17.slot_ref, bf16[128,64,128]{2,1,0:T(8,128)(2,1)S(1)} %collective-permute-done.second_ref, bf16[128,96,128]{2,1,0:T(8,128)(2,1)S(1)} %all_to_all.10.refs_1_.refs_2_.own_ref, bf16[16,256]{1,0:T(8,128)(2,1)S(1)} %copy-done.1, ...), custom_call_target="tpu_custom_call", output_to_operand_aliasing={{}: (5, {})} | custom-call | flops 8589934592 | bytes 9437184 | tf_op jit(solution)/shard_map/correlate_second/pallas_call | solution.py:357
  (6 shorter events, 0.1 us)
Async XLA Ops:
  0.0 16.5 %copy-start.3 = (s32[32]{0:T(128)S(1)}, s32[32]{0:T(128)}, u32[]{:S(2)}) copy-start(s32[32]{0:T(128)} %param.11) | copy-start | bytes 388
  0.0 17.0 %copy-start.2 = (s32[32,16]{0,1:T(8,128)S(1)}, s32[32,16]{0,1:T(8,128)}, u32[]{:S(2)}) copy-start(s32[32,16]{0,1:T(8,128)} %param.10) | copy-start | bytes 6148
  0.0 17.3 %copy-start.4 = (s32[64]{0:T(128)S(1)}, s32[64]{0:T(128)}, u32[]{:S(2)}) copy-start(s32[64]{0:T(128)} %param.12) | copy-start | bytes 772
  7.3 19.0 %all-to-all-start = ((bf16[32,64,128]{2,1,0:T(8,128)(2,1)}), bf16[32,64,128]{2,1,0:T(8,128)(2,1)S(1)}, u32[]{:S(2)}, u32[]{:S(2)}) async-start(bf16[32,64,128]{2,1,0:T(8,128)(2,1)} %front.1), calls=%async_computation | async-start | bytes 1048576 | tf_op jit(solution)/shard_map/all_to_all | solution.py:383
  77.0 1.6 %copy-start = (bf16[2,136,512]{2,1,0:T(8,128)(2,1)S(1)}, bf16[2,136,512]{2,1,0:T(8,128)(2,1)}, u32[]{:S(2)}) copy-start(bf16[2,136,512]{2,1,0:T(8,128)(2,1)} %constant.54.clone.refs_4_.table_ref) | copy-start | bytes 835588
  77.0 1.6 %copy-start.1 = (bf16[16,256]{1,0:T(8,128)(2,1)S(1)}, bf16[16,256]{1,0:T(8,128)(2,1)}, u32[]{:S(2)}) copy-start(bf16[16,256]{1,0:T(8,128)(2,1)} %constant.53.clone.refs_3_.mask_ref) | copy-start | bytes 24580
  77.3 6.1 %collective-permute-start = (bf16[128,64,128]{2,1,0:T(8,128)(2,1)S(1)}, bf16[128,64,128]{2,1,0:T(8,128)(2,1)S(1)}, u32[]{:S(2)}, u32[]{:S(2)}) collective-permute-start(bf16[128,64,128]{2,1,0:T(8,128)(2,1)S(1)} %slice.4), channel_id=1, source_target_pairs={{0,1},{1,0},{2,3},{3,2},{4,5},{5,4},{6,7},{7,6},{8,9},{9,8},{10,11... | collective-permute-start | bytes 6291464 | tf_op jit(solution)/shard_map/ppermute | solution.py:386
